TPU v7x, 32 devices: a whole 2x2x4 slice. The times are simulated.
32 devices in a mesh: seq: 8 (over z, x), tp: 4 (over y, core).
Axes of the slice: x: 2, y: 2, z: 4, core: 2. Of those that a mesh axis runs over, the one named last changes fastest.
Arguments:
- tokens: bfloat16 [2048, 1536], P('seq'), may hold values from -6 to 6
- norm1_gain: bfloat16 [1536], replicated, may hold values from 0.25 to 1.75
- w_query: bfloat16 [1536, 1536], P('tp'), may hold values from -0.15625 to 0.15625
- key_weight: bfloat16 [512, 1536], P('tp'), may hold values from -0.4375 to 0.4375
- value_weight: bfloat16 [512, 1536], P('tp'), may hold values from -0.15625 to 0.15625
- rotated_key_cache: bfloat16 [4, 8, 524288], P(None, 'tp', 'seq'), may hold values from -60 to 60
- stored_value_cache: bfloat16 [4, 8, 524288], P(None, 'tp', 'seq'), may hold values from -6 to 6
- cache_len: int32 [4], replicated, may hold values from 1 to 8192, 16384 in all
- w_out: bfloat16 [1536, 1536], P('tp'), may hold values from -0.15625 to 0.15625
- norm2_gain: bfloat16 [1536], replicated, may hold values from 0.25 to 1.75
- w_router: bfloat16 [1536, 40], replicated, may hold values from -0.0546875 to 0.0546875
- expert_ids: int32 [2048, 8], P('seq'), may hold values from 0 to 39, all different within a row
- w_gate_up: bfloat16 [40, 2, 1536, 512], P('tp', None, 'seq'), may hold values from -0.15625 to 0.15625
- w_down: bfloat16 [40, 512, 1536], P('tp', 'seq'), may hold values from -0.5 to 0.5
Outputs:
- attn_out: bfloat16 [2048, 1536], P('seq')
- expert_out: bfloat16 [2048, 1536], P('seq')
Inputs may be any that keep to these rules, and one draw needn't show every extreme that they name: `cache_len`: request lengths of 1 to 8192; one request fills all 8192 positions. `expert_ids`: each row names 8 different experts; every expert is named.
All inputs are finite; a program needn't handle non-finite values.
Results may differ from a plain program's by a relative error of at most 0.03.
Values may be sent and summed in bfloat16 or wider, within the bound.
A program may use at most 192 MiB of HBM per device.

v0:
```python
import jax
import jax.numpy as jnp
from jax import lax
from jax.sharding import PartitionSpec as P

HEAD_SIZE = 64
FRESH_TOKENS = 512


EPS = 1e-05
THETA = 10000.0
NEGATIVE = -1e30


def combined_all(x, axis, join):
    gathered = jax.tree.map(
        lambda a, kind: lax.all_gather(a.astype(kind), axis),
        x,
        (jnp.bfloat16, jnp.bfloat16, jnp.bfloat16),
    )

    def take(source):
        return jax.tree.map(
            lambda a, own: lax.dynamic_index_in_dim(a, source, 0, False).astype(own.dtype),
            gathered,
            x,
        )

    return lax.fori_loop(
        1, lax.axis_size(axis), lambda source, state: join(state, take(source)), take(0)
    )


def rms_norm(values, gain):
    mean_square = jnp.mean(values * values, axis=-1, keepdims=True)
    return values * lax.rsqrt(mean_square + EPS) * gain.astype(values.dtype)


def apply_rotary(values, positions):
    half_dim = values.shape[-1] // 2
    exponent = jnp.arange(half_dim, dtype=jnp.float32) * (2.0 / values.shape[-1])
    freqs = THETA ** (-exponent)
    angles = positions[:, None] * freqs[None, :]
    cosine = jnp.cos(angles)[:, None, :]
    sine = jnp.sin(angles)[:, None, :]
    first = values[..., :half_dim]
    second = values[..., half_dim:]
    return jnp.concatenate(
        [first * cosine - second * sine, second * cosine + first * sine], axis=-1
    )


def apply_projection(normalized_input, weight):
    return jnp.einsum("td,fd->tf", normalized_input, weight, preferred_element_type=jnp.float32)


def lookup(table, index):
    hits = index[:, None] == jnp.arange(table.shape[0], dtype=jnp.int32)[None, :]
    return jnp.sum(jnp.where(hits, table[None, :], 0), axis=1)


def join_parts(first, second):
    out_a, peak_a, sum_a = first
    out_b, peak_b, sum_b = second
    top = jnp.maximum(peak_a, peak_b)
    factor_a = jnp.exp(peak_a - top)
    factor_b = jnp.exp(peak_b - top)
    return (
        out_a * factor_a[..., None] + out_b * factor_b[..., None],
        top,
        sum_a * factor_a + sum_b * factor_b,
    )


def per_device(
    tokens,
    norm1_gain,
    w_query,
    key_weight,
    value_weight,
    rotated_key_cache,
    stored_value_cache,
    cache_len,
    w_out,
    norm2_gain,
    w_router,
    expert_ids,
    w_gate_up,
    w_down,
):
    tok_rows, width = tokens.shape
    seq_pos = lax.axis_index("seq")
    tp_pos = lax.axis_index("tp")
    local_q = w_query.shape[0] // HEAD_SIZE
    local_kv = key_weight.shape[0] // HEAD_SIZE
    query_group = local_q // local_kv
    requests = rotated_key_cache.shape[0]
    span = rotated_key_cache.shape[2] // HEAD_SIZE
    scale = HEAD_SIZE ** (-0.5)
    inputs = tokens.astype(jnp.float32)
    normalized_input = rms_norm(inputs, norm1_gain).astype(jnp.bfloat16)
    row_ids = seq_pos * tok_rows + jnp.arange(tok_rows, dtype=jnp.int32)
    owners = row_ids // FRESH_TOKENS
    positions = lookup(cache_len, owners) + row_ids % FRESH_TOKENS
    angle_position = positions.astype(jnp.float32)
    query_vector = apply_rotary(
        apply_projection(normalized_input, w_query).reshape(tok_rows, local_q, HEAD_SIZE),
        angle_position,
    ).astype(jnp.bfloat16)
    fresh_key = apply_rotary(
        apply_projection(normalized_input, key_weight).reshape(tok_rows, local_kv, HEAD_SIZE),
        angle_position,
    ).astype(jnp.bfloat16)
    fresh_value = (
        apply_projection(normalized_input, value_weight)
        .astype(jnp.bfloat16)
        .reshape(tok_rows, local_kv, HEAD_SIZE)
    )
    all_query = lax.all_gather(
        query_vector.reshape(tok_rows, local_q * HEAD_SIZE), "seq", axis=0, tiled=True
    )
    cache_pos = seq_pos * span + jnp.arange(span, dtype=jnp.int32)
    key_pos = jnp.concatenate([cache_pos, positions])

    def one_request(request_index):
        length = lax.dynamic_index_in_dim(cache_len, request_index, 0, keepdims=False)
        query_rows = lax.dynamic_slice_in_dim(
            all_query, request_index * FRESH_TOKENS, FRESH_TOKENS, 0
        ).reshape(FRESH_TOKENS, local_kv, query_group, HEAD_SIZE)
        query_pos = length + jnp.arange(FRESH_TOKENS, dtype=jnp.int32)
        prior_keys = jnp.transpose(
            lax.dynamic_index_in_dim(rotated_key_cache, request_index, 0, keepdims=False).reshape(
                local_kv, span, HEAD_SIZE
            ),
            (1, 0, 2),
        )
        prior_values = jnp.transpose(
            lax.dynamic_index_in_dim(stored_value_cache, request_index, 0, keepdims=False).reshape(
                local_kv, span, HEAD_SIZE
            ),
            (1, 0, 2),
        )
        keys = jnp.concatenate([prior_keys, fresh_key], axis=0)
        values = jnp.concatenate([prior_values, fresh_value], axis=0)
        usable = jnp.concatenate([cache_pos < length, owners == request_index])
        allowed = usable[None, :] & (key_pos[None, :] <= query_pos[:, None])
        scores = (
            jnp.einsum("nhgd,khd->hgnk", query_rows, keys, preferred_element_type=jnp.float32)
            * scale
        )
        scores = jnp.where(allowed[None, None], scores, NEGATIVE)
        peak = jnp.max(scores, axis=-1)
        weights = jnp.where(allowed[None, None], jnp.exp(scores - peak[..., None]), 0.0)
        total = jnp.sum(weights, axis=-1)
        mixed = jnp.einsum(
            "hgnk,khd->nhgd",
            weights.astype(jnp.bfloat16),
            values,
            preferred_element_type=jnp.float32,
        )
        return (
            mixed.reshape(FRESH_TOKENS, local_q, HEAD_SIZE),
            jnp.transpose(peak, (2, 0, 1)).reshape(FRESH_TOKENS, local_q),
            jnp.transpose(total, (2, 0, 1)).reshape(FRESH_TOKENS, local_q),
        )

    part_out, part_peak, part_sum = lax.map(one_request, jnp.arange(requests, dtype=jnp.int32))
    total_rows = requests * FRESH_TOKENS
    part_out = part_out.reshape(total_rows, local_q, HEAD_SIZE)
    part_peak = part_peak.reshape(total_rows, local_q)
    part_sum = part_sum.reshape(total_rows, local_q)
    full_out, full_peak, full_sum = combined_all((part_out, part_peak, part_sum), "seq", join_parts)
    own_out = lax.dynamic_slice_in_dim(full_out, seq_pos * tok_rows, tok_rows, 0)
    own_sum = lax.dynamic_slice_in_dim(full_sum, seq_pos * tok_rows, tok_rows, 0)
    heads_out = (
        (own_out / own_sum[..., None]).astype(jnp.bfloat16).reshape(tok_rows, local_q * HEAD_SIZE)
    )
    attn_part = jnp.dot(heads_out, w_out, preferred_element_type=jnp.float32)
    attn = lax.psum(attn_part.astype(jnp.bfloat16), "tp").astype(jnp.float32)
    attn_out = attn.astype(jnp.bfloat16)
    normed2 = rms_norm(inputs + attn, norm2_gain).astype(jnp.bfloat16)
    logits = jnp.dot(normed2, w_router, preferred_element_type=jnp.float32)
    experts_all = w_router.shape[1]
    picked_all = expert_ids[:, :, None] == jnp.arange(experts_all, dtype=jnp.int32)[None, None, :]
    chosen = jnp.sum(jnp.where(picked_all, logits[:, None, :], 0.0), axis=-1)
    gates = jax.nn.softmax(chosen, axis=-1)
    local_experts = w_gate_up.shape[0]
    local_ids = tp_pos * local_experts + jnp.arange(local_experts, dtype=jnp.int32)
    picked = expert_ids[:, :, None] == local_ids[None, None, :]
    share = jnp.sum(jnp.where(picked, gates[:, :, None], 0.0), axis=1)
    both = jnp.einsum(
        "td,ecdf->tecf",
        normed2,
        lax.all_gather(w_gate_up, "seq", axis=2, tiled=True),
        preferred_element_type=jnp.float32,
    )
    hidden = (jax.nn.silu(both[:, :, 0]) * both[:, :, 1] * share[:, :, None]).astype(jnp.bfloat16)
    moe_part = jnp.einsum(
        "tef,efd->td",
        hidden,
        lax.all_gather(w_down, "seq", axis=1, tiled=True),
        preferred_element_type=jnp.float32,
    )
    expert_out = lax.psum(moe_part.astype(jnp.bfloat16), "tp")
    return (attn_out, expert_out)


def solution(mesh):
    return jax.shard_map(
        per_device,
        mesh=mesh,
        in_specs=(
            P("seq", None),
            P(),
            P("tp", None),
            P("tp", None),
            P("tp", None),
            P(None, "tp", "seq"),
            P(None, "tp", "seq"),
            P(),
            P("tp", None),
            P(),
            P(),
            P("seq", None),
            P("tp", None, "seq", None),
            P("tp", "seq", None),
        ),
        out_specs=(P("seq", None), P("seq", None)),
        check_vma=False,
    )
```

profile of v0, /device:TPU:0, one launch (start us, length us, event | category | flops | bytes accessed | tf_op | source)
XLA Modules:
  0.0 1429.9 jit_solution(5135392663269853709)
XLA Ops:
  15.7 45.8 %all-gather.5.cloned.1.call-done = bf16[2048,384]{0,1:T(8,128)(2,1)} async-done(((bf16[256,384]{0,1:T(8,128)(2,1)}), bf16[2048,384]{0,1:T(8,128)(2,1)}) %all-gather.5.cloned.1.call-update) | async-done | bytes 1572880 | tf_op jit(solution)/shard_map/all_gather | solution.py:119
  61.5 112.0 %while.35 = (s32[]{:T(128)}, bf16[4,512,6,64]{1,3,2,0:T(8,128)(2,1)}, bf16[4,512,6]{1,2,0:T(8,128)(2,1)S(1)}, bf16[4,512,6]{1,2,0:T(8,128)(2,1)S(1)}, s32[4]{0:T...) while((s32[]{:T(128)}, ...), condition=%wide.region_5.6_spmd.clone, body=%wide.region_2.5_spmd.clone.sunk | while | flops 1060374528 | bytes 119003984 | solution.py:167
  71.0 2.6 fusion.77
  73.6 3.8 fusion.79
  80.9 7.9 fusion.78
  99.0 2.6 fusion.77
  101.6 3.8 fusion.79
  108.8 7.9 fusion.78
  127.0 2.6 fusion.77
  129.6 3.8 fusion.79
  136.9 7.9 fusion.78
  157.6 3.8 fusion.79
  164.9 7.9 fusion.78
  173.5 2.6 copy.79
  178.6 31.7 %all_gather.23 = bf16[8,2048,6]{1,2,0:T(8,128)(2,1)S(1)} all-gather(bf16[1,2048,6]{1,2,0:T(8,128)(2,1)S(1)} %bitcast.154), channel_id=1, replica_groups=mesh['seq'=8,'tp'=4] {'seq'}, dimensions={0}, use_global_device_ids=true | all-gather | bytes 221184 | tf_op jit(solution)/shard_map/all_gather | solution.py:17
  211.8 32.3 %all_gather.24 = bf16[8,2048,6]{1,2,0:T(8,128)(2,1)S(1)} all-gather(bf16[1,2048,6]{1,2,0:T(8,128)(2,1)S(1)} %bitcast.155), channel_id=1, replica_groups=mesh['seq'=8,'tp'=4] {'seq'}, dimensions={0}, use_global_device_ids=true | all-gather | bytes 221184 | tf_op jit(solution)/shard_map/all_gather | solution.py:17
  244.4 112.8 %all-gather.7.cloned.1.call-done = bf16[8,2048,6,64]{1,3,2,0:T(8,128)(2,1)} async-done(((bf16[1,2048,6,64]{1,3,2,0:T(8,128)(2,1)}), bf16[8,2048,6,64]{1,3,2,0:T(8,128)(2,1)}) %all-gather.7.cloned.1.call-update) | async-done | bytes 12582928 | tf_op jit(solution)/shard_map/all_gather | solution.py:17
  357.2 3.5 fusion.35
  360.7 6.6 copy.80
  367.3 147.2 %while.34 = (s32[]{:T(128)}, f32[2048,6,64]{2,1,0:T(8,128)}, f32[2048,6]{1,0:T(8,128)}, f32[2048,6]{1,0:T(8,128)S(1)}, bf16[8,2048,6]{1,2,0:T(8,128)(2,1)S(1)}, ...) while((s32[]{:T(128)}, f32[2048,6,64]{2,1,0:T(8,128)}, ...), condition=%wide.region_7.8_spmd, body=%wide.region_6.7_spmd.sunk | while | flops 3244037 | bytes 18334016 | solution.py:29
  368.6 3.2 fusion.72
  374.3 4.2 copy.103
  378.6 9.7 fusion.73
  389.7 3.2 fusion.72
  395.3 4.2 copy.103
  399.6 9.7 fusion.73
  410.7 3.2 fusion.72
  416.4 4.2 copy.103
  420.6 9.7 fusion.73
  431.7 3.2 fusion.72
  437.4 4.2 copy.103
  441.7 9.7 fusion.73
  452.7 3.2 fusion.72
  458.4 4.2 copy.103
  462.7 9.7 fusion.73
  473.8 3.2 fusion.72
  479.5 4.2 copy.103
  483.7 9.7 fusion.73
  494.8 3.2 fusion.72
  500.5 4.2 copy.103
  504.8 9.7 fusion.73
  514.5 6.3 copy.86
  524.8 31.7 %all-reduce.3.cloned.1.call-done = bf16[256,1536]{1,0:T(8,128)(2,1)} async-done(((bf16[256,1536]{1,0:T(8,128)(2,1)}), bf16[256,1536]{1,0:T(8,128)(2,1)}) %all-reduce.3.cloned.1.call-update) | async-done | bytes 786448 | tf_op jit(solution)/shard_map/psum | solution.py:179
  560.0 596.4 %all-gather.9.cloned.1.call-done = bf16[10,2,1536,512]{3,2,1,0:T(8,128)(2,1)} async-done(((bf16[10,2,192,512]{3,2,1,0:T(8,128)(2,1)}), bf16[10,2,1536,512]{3,2,1,0:T(8,128)(2,1)}) %all-gather.9.cloned.1.call-update) | async-done | bytes 31457296 | tf_op jit(solution)/shard_map/all_gather | solution.py:194
  1156.3 17.0 %fusion.36 = f32[256,10,2,512]{3,0,2,1:T(8,128)} fusion(bf16[10,2,1536,512]{3,2,1,0:T(8,128)(2,1)} %all-gather.9.cloned.1.call-done, bf16[256,1536]{1,0:T(8,128)(2,1)S(1)} %multiply_convert_fusion), kind=kOutput, calls=%fused_computation.67 | convolution fusion | flops 8053063680 | bytes 42729472 | tf_op jit(solution)/shard_map/td,ecdf->tecf/dot_general | solution.py:191
  1173.3 199.8 %all-gather.11.cloned.1.call-done = bf16[10,512,1536]{2,1,0:T(8,128)(2,1)} async-done(((bf16[10,64,1536]{2,1,0:T(8,128)(2,1)}), bf16[10,512,1536]{2,1,0:T(8,128)(2,1)}) %all-gather.11.cloned.1.call-update) | async-done | bytes 15728656 | tf_op jit(solution)/shard_map/all_gather | solution.py:201
  1373.2 13.9 fusion.29
  1387.1 33.0 %all-reduce.5.cloned.1.call-done = bf16[256,1536]{1,0:T(8,128)(2,1)} async-done(((bf16[256,1536]{1,0:T(8,128)(2,1)}), bf16[256,1536]{1,0:T(8,128)(2,1)}) %all-reduce.5.cloned.1.call-update) | async-done | bytes 786448 | tf_op jit(solution)/shard_map/psum | solution.py:204
  (266 shorter events, 96.3 us)
Async XLA Ops:
  7.2 514.8 %copy-start = (bf16[384,1536]{1,0:T(8,128)(2,1)S(1)}, bf16[384,1536]{1,0:T(8,128)(2,1)}, u32[]{:S(2)}) copy-start(bf16[384,1536]{1,0:T(8,128)(2,1)} %param.26) | copy-start | bytes 3538948
  7.2 54.3 %copy-start.14 = (s32[4]{0:T(128)S(1)}, s32[4]{0:T(128)}, u32[]{:S(2)}) copy-start(s32[4]{0:T(128)} %param.25) | copy-start | bytes 52
  7.2 8.0 copy-start.4
  7.2 8.0 copy-start.15
  7.2 54.3 %all-gather.5.cloned.1.call-start = ((), (), s32[]{:S(2)}) async-start(), calls=%async_computation | async-start | bytes 1769472 | tf_op jit(solution)/shard_map/all_gather | solution.py:119
  13.4 343.9 %all-gather.7.cloned.1.call-start = ((), (), s32[]{:S(2)}) async-start(), calls=%async_computation.1 | async-start | bytes 14155776 | tf_op jit(solution)/shard_map/all_gather | solution.py:17
  73.6 5.5 copy-start.1
  101.6 5.5 copy-start.1
  129.6 5.5 copy-start.1
  157.6 5.5 copy-start.1
  178.6 377.9 %all-reduce.3.cloned.1.call-start = ((), (), s32[]{:S(2)}) async-start(), calls=%async_computation.2 | async-start | bytes 1572864 | tf_op jit(solution)/shard_map/psum | solution.py:179
  367.3 1.0 copy-start.7
  371.8 1.0 copy-start.2
  378.6 9.7 copy-start.3
  378.6 9.7 copy-start.8
  378.6 9.7 copy-start.10
  388.3 1.0 copy-start.7
  399.6 9.7 copy-start.3
  399.6 9.7 copy-start.8
  399.6 9.7 copy-start.10
  409.3 1.0 copy-start.7
  420.6 9.7 copy-start.3
  420.6 9.7 copy-start.8
  420.6 9.7 copy-start.10
  430.4 1.0 copy-start.7
  441.7 9.7 copy-start.3
  441.7 9.7 copy-start.8
  441.7 9.7 copy-start.10
  451.4 1.0 copy-start.7
  462.7 9.7 copy-start.3
  462.7 9.7 copy-start.8
  462.7 9.7 copy-start.10
  472.4 1.0 copy-start.7
  483.7 9.7 copy-start.3
  483.7 9.7 copy-start.8
  483.7 9.7 copy-start.10
  493.5 1.0 copy-start.7
  504.7 9.7 copy-start.3
  504.8 9.7 copy-start.8
  504.8 9.7 copy-start.10
  520.8 3.9 copy-start.13
  520.8 35.7 %copy-start.5 = (bf16[256,1536]{1,0:T(8,128)(2,1)S(1)}, bf16[256,1536]{1,0:T(8,128)(2,1)}, u32[]{:S(2)}) copy-start(bf16[256,1536]{1,0:T(8,128)(2,1)} %param.18) | copy-start | bytes 2359300
  523.5 35.9 %copy-start.11 = (bf16[1536,40]{0,1:T(8,128)(2,1)S(1)}, bf16[1536,40]{0,1:T(8,128)(2,1)}, u32[]{:S(2)}) copy-start(bf16[1536,40]{0,1:T(8,128)(2,1)} %param.28) | copy-start | bytes 368644
  523.5 36.3 %copy-start.12 = (s32[256,8]{0,1:T(8,128)S(1)}, s32[256,8]{0,1:T(8,128)}, u32[]{:S(2)}) copy-start(s32[256,8]{0,1:T(8,128)} %param.29) | copy-start | bytes 24580
  523.5 632.8 %all-gather.9.cloned.1.call-start = ((), (), s32[]{:S(2)}) async-start(), calls=%async_computation.3 | async-start | bytes 35389440 | tf_op jit(solution)/shard_map/all_gather | solution.py:194
  524.1 849.1 %all-gather.11.cloned.1.call-start = ((), (), s32[]{:S(2)}) async-start(), calls=%async_computation.4 | async-start | bytes 17694720 | tf_op jit(solution)/shard_map/all_gather | solution.py:201
  524.7 895.4 %all-reduce.5.cloned.1.call-start = ((), (), s32[]{:S(2)}) async-start(), calls=%async_computation.5 | async-start | bytes 1572864 | tf_op jit(solution)/shard_map/psum | solution.py:204
  1173.3 246.8 %copy-start.6 = (bf16[256,1536]{1,0:T(8,128)(2,1)S(1)}, bf16[256,1536]{1,0:T(8,128)(2,1)}, u32[]{:S(2)}) copy-start(bf16[256,1536]{1,0:T(8,128)(2,1)} %all-reduce.3.cloned.1.call-done) | copy-start | bytes 2359300
  (13 other events, 10.9 us)
Sparse Core Ops, SparseCore 0:
  13.5 47.9 all-gather.4
  178.7 178.4 all-gather.6
  523.6 32.8 all-reduce.2
  557.9 598.4 all-gather.8
  1158.4 214.7 all-gather.10
  1387.2 32.7 all-reduce.4
where the time goes:
time: 1430 us
  waiting for transfers between devices  1020 us (71%)
  other arithmetic  129 us (9%)
  local copies, waits for them, and re-layouts  112 us (8%)
  matrix products  78.9 us (6%)
  blocking collectives  64 us (4%)
  between operations  14.4 us (1%)
    all_gather x1, waiting for transfers between devices, per_device(): lax.all_gather(w_gate_up, 'seq', axis=2, tiled=True)  596 us
    all_gather x1, waiting for transfers between devices, per_device(): lax.all_gather(w_down, 'seq', axis=1, tiled=True)  200 us
    all_gather x1, waiting for transfers between devices, combined_all(): lax.all_gather(a.astype(kind), axis)  113 us
    add x7, other arithmetic, join_parts(): out_a * factor_a[..., None] + out_b * factor_b[..., None]  67.9 us
    all_gather x2, blocking collectives, combined_all(): lax.all_gather(a.astype(kind), axis)  64 us
    all_gather x1, waiting for transfers between devices, per_device(): lax.all_gather(query_vector.reshape(tok_rows, local_q * HEAD_SIZE), 'seq'...  45.8 us
    dynamic_slice x35, local copies, waits for them, and re-layouts, take(): lax.dynamic_index_in_dim(a, source, 0, False).astype(own.dtype)  44.7 us
    psum x1, waiting for transfers between devices, per_device(): expert_out = lax.psum(moe_part.astype(jnp.bfloat16), 'tp')  33 us
  transfers between devices with their start and end apart: 6, of which 6 were waited for; matrix products, arithmetic and copies ran while one was open for 2% of the time, Pallas kernels for 0%

commit v1 on v0

v1 whole, which is shorter than its diff:
```python
import jax
import jax.numpy as jnp
from jax import lax
from jax.experimental import pallas as pl
from jax.experimental.pallas import tpu as pltpu
from jax.sharding import PartitionSpec as P

HEAD_SIZE = 64
FRESH_TOKENS = 512


EPS = 1e-05
THETA = 10000.0
NEGATIVE = -1e30


def rms_norm(values, gain):
    mean_square = jnp.mean(values * values, axis=-1, keepdims=True)
    return values * lax.rsqrt(mean_square + EPS) * gain.astype(values.dtype)


def apply_rotary(values, positions):
    half_dim = values.shape[-1] // 2
    exponent = jnp.arange(half_dim, dtype=jnp.float32) * (2.0 / values.shape[-1])
    freqs = THETA ** (-exponent)
    angles = positions[:, None] * freqs[None, :]
    cosine = jnp.cos(angles)[:, None, :]
    sine = jnp.sin(angles)[:, None, :]
    first = values[..., :half_dim]
    second = values[..., half_dim:]
    return jnp.concatenate(
        [first * cosine - second * sine, second * cosine + first * sine], axis=-1
    )


def apply_projection(normalized_input, weight):
    return jnp.einsum("td,fd->tf", normalized_input, weight, preferred_element_type=jnp.float32)


def lookup(table, index):
    hits = index[:, None] == jnp.arange(table.shape[0], dtype=jnp.int32)[None, :]
    return jnp.sum(jnp.where(hits, table[None, :], 0), axis=1)


def attend_kernel(info, q_ref, k_ref, v_ref, fk_ref, fv_ref, out_ref, peak_ref, sum_ref, acc_ref):
    group, rows = out_ref.shape[1], out_ref.shape[2]
    pairs = k_ref.shape[2]
    columns = q_ref.shape[1]
    head = pl.program_id(0)
    dest = pl.program_id(1)
    me = info[0]
    per = FRESH_TOKENS // rows
    length = info[1 + dest // per]
    base = me * (2 * pairs)
    col = lax.broadcasted_iota(jnp.int32, (columns, 128), 0)
    lane = lax.broadcasted_iota(jnp.int32, (columns, 128), 1)
    out_lane = lax.broadcasted_iota(jnp.int32, (rows, 128), 1)
    has_cache = base < length
    has_fresh = (dest // per == me // per) & (dest >= me)
    nt = (((1,), (1,)), ((), ()))

    def pick(g, odd):
        start = (head * group + g) * HEAD_SIZE
        hit = (col == start + lane - odd * HEAD_SIZE) & (lane // HEAD_SIZE == odd)
        select = jnp.where(hit, HEAD_SIZE ** (-0.5), 0.0).astype(jnp.bfloat16)
        return jnp.dot(q_ref[...], select, preferred_element_type=jnp.float32).astype(jnp.bfloat16)

    @pl.when(jnp.logical_not(has_cache))
    def _():
        peak_ref[...] = jnp.full_like(peak_ref, NEGATIVE)
        sum_ref[...] = jnp.zeros_like(sum_ref)
        acc_ref[...] = jnp.zeros_like(acc_ref)

    @pl.when(has_cache)
    def _():
        keys = k_ref[0, 0]
        values = v_ref[0, 0]
        even_pos = base + 2 * lax.broadcasted_iota(jnp.int32, (1, pairs), 1)
        even_bias = jnp.where(even_pos < length, 0.0, NEGATIVE)
        odd_bias = jnp.where(even_pos + 1 < length, 0.0, NEGATIVE)
        for g in range(group):
            even = lax.dot_general(pick(g, 0), keys, nt, preferred_element_type=jnp.float32) + even_bias
            odd = lax.dot_general(pick(g, 1), keys, nt, preferred_element_type=jnp.float32) + odd_bias
            peak = jnp.max(jnp.maximum(even, odd), axis=1, keepdims=True)
            even = jnp.exp(even - peak)
            odd = jnp.exp(odd - peak)
            total = jnp.sum(even + odd, axis=1, keepdims=True)
            mix_even = jnp.dot(even.astype(jnp.bfloat16), values, preferred_element_type=jnp.float32)
            mix_odd = jnp.dot(odd.astype(jnp.bfloat16), values, preferred_element_type=jnp.float32)
            mixed = jnp.where(out_lane < HEAD_SIZE, mix_even, mix_odd)
            peak_ref[g] = jnp.broadcast_to(peak, (rows, 128))
            sum_ref[g] = jnp.broadcast_to(total, (rows, 128))
            acc_ref[g] = mixed

    @pl.when(has_fresh)
    def _():
        row_q = dest * rows + lax.broadcasted_iota(jnp.int32, (rows, rows), 0)
        row_k = me * rows + lax.broadcasted_iota(jnp.int32, (rows, rows), 1)
        bias = jnp.where(row_k <= row_q, 0.0, NEGATIVE)
        for g in range(group):
            score = lax.dot_general(pick(g, 0), fk_ref[0], nt, preferred_element_type=jnp.float32) + bias
            old = peak_ref[g][:, :1]
            peak = jnp.maximum(old, jnp.max(score, axis=1, keepdims=True))
            weight = jnp.exp(score - peak)
            factor = jnp.exp(old - peak)
            total = sum_ref[g][:, :1] * factor + jnp.sum(weight, axis=1, keepdims=True)
            mix = jnp.dot(weight.astype(jnp.bfloat16), fv_ref[0], preferred_element_type=jnp.float32)
            acc_ref[g] = acc_ref[g] * factor + mix
            peak_ref[g] = jnp.broadcast_to(peak, (rows, 128))
            sum_ref[g] = jnp.broadcast_to(total, (rows, 128))

    for g in range(group):
        acc = acc_ref[g]
        acc = acc + pltpu.roll(acc, HEAD_SIZE, 1)
        total = sum_ref[g]
        some = total > 0.0
        safe = jnp.where(some, total, 1.0)
        level = jnp.where(some, peak_ref[g] + jnp.log(safe), NEGATIVE)
        high = level.astype(jnp.bfloat16).astype(jnp.float32)
        middle = (level - high).astype(jnp.bfloat16).astype(jnp.float32)
        low = level - high - middle
        tail = jnp.where(out_lane == HEAD_SIZE, high, jnp.where(out_lane == HEAD_SIZE + 1, middle, low))
        out_ref[0, g] = jnp.where(out_lane < HEAD_SIZE, acc / safe, tail).astype(out_ref.dtype)


def attend(info, query, keys, values, fresh_key, fresh_value, rows, local_q):
    local_kv, pairs = keys.shape[1], keys.shape[2]
    group = local_q // local_kv
    per = FRESH_TOKENS // rows
    dests = query.shape[0] // rows
    cache_spec = pl.BlockSpec((1, 1, pairs, 128), lambda j, d, info: (d // per, j, 0, 0))
    fresh_spec = pl.BlockSpec((1, rows, 128), lambda j, d, info: (j, 0, 0))
    return pl.pallas_call(
        attend_kernel,
        grid_spec=pltpu.PrefetchScalarGridSpec(
            num_scalar_prefetch=1,
            grid=(local_kv, dests),
            in_specs=[
                pl.BlockSpec((rows, local_q * HEAD_SIZE), lambda j, d, info: (d, 0)),
                cache_spec,
                cache_spec,
                fresh_spec,
                fresh_spec,
            ],
            out_specs=pl.BlockSpec((1, group, rows, 128), lambda j, d, info: (d, j, 0, 0)),
            scratch_shapes=[pltpu.VMEM((group, rows, 128), jnp.float32)] * 3,
        ),
        out_shape=jax.ShapeDtypeStruct((dests, local_q, rows, 128), jnp.bfloat16),
        compiler_params=pltpu.CompilerParams(vmem_limit_bytes=40 * 1024 * 1024),
        cost_estimate=pl.CostEstimate(
            flops=8 * query.size * pairs * 2, bytes_accessed=16 << 20, transcendentals=query.size * pairs // 32
        ),
    )(info, query, keys, values, fresh_key, fresh_value)


def per_device(
    tokens,
    norm1_gain,
    w_query,
    key_weight,
    value_weight,
    rotated_key_cache,
    stored_value_cache,
    cache_len,
    w_out,
    norm2_gain,
    w_router,
    expert_ids,
    w_gate_up,
    w_down,
):
    tok_rows, width = tokens.shape
    seq_pos = lax.axis_index("seq")
    tp_pos = lax.axis_index("tp")
    local_q = w_query.shape[0] // HEAD_SIZE
    local_kv = key_weight.shape[0] // HEAD_SIZE
    requests = rotated_key_cache.shape[0]
    span = rotated_key_cache.shape[2] // HEAD_SIZE
    inputs = tokens.astype(jnp.float32)
    devices = lax.axis_size("seq")
    local_experts, _, own_width, hidden_size = w_gate_up.shape
    own_hidden = hidden_size // devices
    own_gate_up = jnp.transpose(
        w_gate_up.reshape(local_experts, 2, own_width, devices, own_hidden), (3, 2, 1, 0, 4)
    ).reshape(width, 2 * local_experts * own_hidden)
    own_gate_up = lax.all_to_all(own_gate_up, "seq", 0, 0, tiled=True)
    normalized_input = rms_norm(inputs, norm1_gain).astype(jnp.bfloat16)
    row_ids = seq_pos * tok_rows + jnp.arange(tok_rows, dtype=jnp.int32)
    owners = row_ids // FRESH_TOKENS
    positions = lookup(cache_len, owners) + row_ids % FRESH_TOKENS
    angle_position = positions.astype(jnp.float32)
    query_vector = apply_rotary(
        apply_projection(normalized_input, w_query).reshape(tok_rows, local_q, HEAD_SIZE),
        angle_position,
    ).astype(jnp.bfloat16)
    fresh_key = apply_rotary(
        apply_projection(normalized_input, key_weight).reshape(tok_rows, local_kv, HEAD_SIZE),
        angle_position,
    ).astype(jnp.bfloat16)
    fresh_value = (
        apply_projection(normalized_input, value_weight)
        .astype(jnp.bfloat16)
        .reshape(tok_rows, local_kv, HEAD_SIZE)
    )
    all_query = lax.all_gather(
        query_vector.reshape(tok_rows, local_q * HEAD_SIZE), "seq", axis=0, tiled=True
    )
    paired = (requests, local_kv, span // 2, 2 * HEAD_SIZE)
    pad = ((0, 0), (0, 0), (0, HEAD_SIZE))
    parts = attend(
        jnp.concatenate([seq_pos[None].astype(jnp.int32), cache_len]),
        all_query,
        rotated_key_cache.reshape(paired),
        stored_value_cache.reshape(paired),
        jnp.pad(jnp.transpose(fresh_key, (1, 0, 2)), pad),
        jnp.pad(jnp.transpose(fresh_value, (1, 0, 2)), pad),
        tok_rows,
        local_q,
    )
    parts = lax.all_to_all(parts, "seq", 0, 0, tiled=True).astype(jnp.float32)
    level = jnp.sum(parts[..., HEAD_SIZE : HEAD_SIZE + 3], axis=-1, keepdims=True)
    factor = jnp.exp(level - jnp.max(level, axis=0, keepdims=True))
    heads_out = jnp.sum(parts[..., :HEAD_SIZE] * factor, axis=0) / jnp.sum(factor, axis=0)
    attn_part = jnp.einsum(
        "htd,hdf->tf",
        heads_out.astype(jnp.bfloat16),
        w_out.reshape(local_q, HEAD_SIZE, width),
        preferred_element_type=jnp.float32,
    )
    attn = lax.psum(attn_part.astype(jnp.bfloat16), "tp").astype(jnp.float32)
    attn_out = attn.astype(jnp.bfloat16)
    normed2 = rms_norm(inputs + attn, norm2_gain).astype(jnp.bfloat16)
    logits = jnp.dot(normed2, w_router, preferred_element_type=jnp.float32)
    experts_all = w_router.shape[1]
    picked_all = expert_ids[:, :, None] == jnp.arange(experts_all, dtype=jnp.int32)[None, None, :]
    chosen = jnp.sum(jnp.where(picked_all, logits[:, None, :], 0.0), axis=-1)
    gates = jax.nn.softmax(chosen, axis=-1)
    local_ids = tp_pos * local_experts + jnp.arange(local_experts, dtype=jnp.int32)
    picked = expert_ids[:, :, None] == local_ids[None, None, :]
    share = jnp.sum(jnp.where(picked, gates[:, :, None], 0.0), axis=1)
    share_high = lax.reduce_precision(share, 8, 7)
    packed = jnp.concatenate(
        [
            normed2,
            share_high.astype(jnp.bfloat16),
            (share - share_high).astype(jnp.bfloat16),
            jnp.zeros((tok_rows, 128 - 2 * local_experts), jnp.bfloat16),
        ],
        axis=1,
    )
    packed = lax.all_gather(packed, "seq", axis=0, tiled=True)
    units = local_experts * own_hidden
    unit_expert = jnp.arange(units, dtype=jnp.int32) // own_hidden
    lanes = jnp.arange(128, dtype=jnp.int32)
    spread = (lanes[:, None] % local_experts == unit_expert[None, :]) & (lanes[:, None] < 2 * local_experts)
    share_all = jnp.dot(packed[:, width:], spread.astype(jnp.bfloat16), preferred_element_type=jnp.float32)
    both = jnp.dot(packed[:, :width], own_gate_up, preferred_element_type=jnp.float32)
    hidden = (jax.nn.silu(both[:, :units]) * both[:, units:] * share_all).astype(jnp.bfloat16)
    moe_part = jnp.dot(hidden, w_down.reshape(units, width), preferred_element_type=jnp.float32)
    moe_part = lax.psum_scatter(moe_part.astype(jnp.bfloat16), "seq", scatter_dimension=0, tiled=True)
    expert_out = lax.psum(moe_part, "tp")
    return (attn_out, expert_out)


def solution(mesh):
    return jax.shard_map(
        per_device,
        mesh=mesh,
        in_specs=(
            P("seq", None),
            P(),
            P("tp", None),
            P("tp", None),
            P("tp", None),
            P(None, "tp", "seq"),
            P(None, "tp", "seq"),
            P(),
            P("tp", None),
            P(),
            P(),
            P("seq", None),
            P("tp", None, "seq", None),
            P("tp", "seq", None),
        ),
        out_specs=(P("seq", None), P("seq", None)),
        check_vma=False,
    )
```

time: 1430 us -> 609 us (0.43)
  waiting for transfers between devices: 1020 us -> 375 us
  other arithmetic: 129 us -> 16.6 us
  local copies, waits for them, and re-layouts: 112 us -> 38.6 us
  Pallas kernels: 0 us -> 51.8 us
  matrix products: 78.9 us -> 32.5 us
    all_gather x3 -> x1, waiting for transfers between devices: 909 us -> 7.29 us  [per_device(): packed = lax.all_gather(packed, 'seq', axis=0, tiled=True)]
    all_to_all x0 -> x1, waiting for transfers between devices: none -> 146 us  [per_device(): own_gate_up = lax.all_to_all(own_gate_up, 'seq', 0, 0, tiled=True)]
    reduce_scatter x0 -> x1, waiting for transfers between devices: none -> 116 us  [per_device(): lax.psum_scatter(moe_part.astype(jnp.bfloat16), 'seq', scatter_dimension=...]
    add x19 -> x0, other arithmetic: 92.7 us -> none  [the longest x7 67.9 us: join_parts(): out_a * factor_a[..., None] + out_b * factor_b[..., None]]
    all_to_all x0 -> x1, blocking collectives: none -> 73 us  [per_device(): parts = lax.all_to_all(parts, 'seq', 0, 0, tiled=True).astype(jnp.float32)]
    all_gather x2 -> x0, blocking collectives: 64 us -> none  [combined_all(): lax.all_gather(a.astype(kind), axis)]
    dynamic_slice x57 -> x0, local copies, waits for them, and re-layouts: 63 us -> none  [the longest x35 44.7 us: take(): lax.dynamic_index_in_dim(a, source, 0, False).astype(own.dtype)]
    pallas_call x0 -> x1, Pallas kernels: none -> 51.8 us  [attend(): pl.pallas_call(attend_kernel, grid_spec=pltpu.PrefetchScalarGridSpec(num_...]
  transfers between devices with their start and end apart: 6 -> 6, of which waited for: 6 -> 6; matrix products, arithmetic and copies ran while one was open for 2% -> 5% of each run, Pallas kernels for 0% -> 0%
where the time goes in v1:
time: 609 us; the launch traced here: 607 us
  waiting for transfers between devices  375 us (62%)
  blocking collectives  73 us (12%)
  Pallas kernels  51.8 us (9%)
  local copies, waits for them, and re-layouts  38.6 us (6%)
  matrix products  32.5 us (5%)
  other arithmetic  16.6 us (3%)
  between operations  14.1 us (2%)
    all_to_all x1, waiting for transfers between devices, per_device(): own_gate_up = lax.all_to_all(own_gate_up, 'seq', 0, 0, tiled=True)  146 us
    reduce_scatter x1, waiting for transfers between devices, per_device(): lax.psum_scatter(moe_part.astype(jnp.bfloat16), 'seq', scatter_dimension=...  116 us
    all_to_all x1, blocking collectives, per_device(): parts = lax.all_to_all(parts, 'seq', 0, 0, tiled=True).astype(jnp.float32)  73 us
    pallas_call x1, Pallas kernels, attend(): pl.pallas_call(attend_kernel, grid_spec=pltpu.PrefetchScalarGridSpec(num_...  51.8 us
    all_gather x1, waiting for transfers between devices, per_device(): lax.all_gather(query_vector.reshape(tok_rows, local_q * HEAD_SIZE), 'seq'...  36.8 us
    psum x1, waiting for transfers between devices, per_device(): expert_out = lax.psum(moe_part, 'tp')  36 us
    psum x1, waiting for transfers between devices, per_device(): attn = lax.psum(attn_part.astype(jnp.bfloat16), 'tp').astype(jnp.float32)  32.9 us
    unnamed x27, local copies, waits for them, and re-layouts  16.1 us
  transfers between devices with their start and end apart: 6, of which 6 were waited for; matrix products, arithmetic and copies ran while one was open for 5% of the time, Pallas kernels for 0%

profile of v1, /device:TPU:0, one launch (start us, length us, event | category | flops | bytes accessed | tf_op | source)
XLA Modules:
  0.0 607.4 jit_solution(14964913529847808712)
XLA Ops:
  7.2 1.5 fusion.6
  8.8 0.8 select_reduce_fusion.2
  9.6 0.7 convert_element_type.61
  10.3 0.2 multiply_cosine_fusion
  10.5 2.1 fusion.35
  12.7 0.8 copy.72
  13.6 0.1 copy.74
  13.7 0.1 copy.76
  13.8 1.5 convolution_convert_fusion.1
  15.2 0.1 copy.77
  15.4 1.5 fusion.33
  16.9 0.1 copy.87
  17.0 0.1 copy.86
  17.3 0.1 maximum_bitcast_fusion
  17.4 2.6 reshape.231.k_ref
  20.0 3.7 reshape.232.v_ref
  23.8 36.8 %all-gather.3.cloned.1.call-done.q_ref = bf16[2048,384]{1,0:T(8,128)(2,1)} async-done(((bf16[256,384]{1,0:T(8,128)(2,1)}), bf16[2048,384]{1,0:T(8,128)(2,1)}) %all-gather.3.cloned.1.call-update) | async-done | bytes 1572880 | tf_op jit(solution)/shard_map/all_gather | solution.py:205
  60.6 1.2 copy-done.1
  61.8 1.4 copy-done.2
  63.2 51.8 %shard_map.149 = bf16[8,6,256,128]{3,2,1,0:T(8,128)(2,1)S(1)} custom-call(s32[5]{0:T(128)S(1)} %pad_add_fusion.info, bf16[2048,384]{1,0:T(8,128)(2,1)S(1)} %copy-done.2, bf16[4,2,512,128]{3,2,1,0:T(8,128)(2,1)S(1)} %reshape.231.k_ref, bf16[4,2,512,128]{3,2,1,0:T(8,128)(2,1)S(1)} %copy-done.1, bf16[2,256,128]{2,1,0:T(8,128)(2,1)S(1)} %pad.7.fk_ref, ...), custom_call_target="tpu_custom_call" | custom-call | flops 6442450944 | bytes 16777216 | tf_op jit(solution)/shard_map/pallas_call | solution.py:133
  115.0 73.0 %all_to_all.17 = bf16[8,6,256,128]{3,2,1,0:T(8,128)(2,1)S(1)} all-to-all(bf16[8,6,256,128]{3,2,1,0:T(8,128)(2,1)S(1)} %shard_map.149), channel_id=1, replica_groups=mesh['seq'=8,'tp'=4] {'seq'}, dimensions={0} | all-to-all | bytes 6291456 | tf_op jit(solution)/shard_map/all_to_all | solution.py:220
  188.0 0.8 convert_element_type.66
  188.8 2.7 copy-done.3
  191.4 3.3 slice_reduce_fusion
  194.8 4.6 fusion.2
  199.4 1.7 fusion.5
  201.1 0.2 all-gather.5.cloned.1.call-start
  201.4 0.5 iota_add_fusion.1
  201.9 32.9 %all-reduce.5.cloned.1.call-done = bf16[256,1536]{1,0:T(8,128)(2,1)} async-done(((bf16[256,1536]{1,0:T(8,128)(2,1)}), bf16[256,1536]{1,0:T(8,128)(2,1)}) %all-reduce.5.cloned.1.call-update) | async-done | bytes 786448 | tf_op jit(solution)/shard_map/psum | solution.py:230
  234.8 1.5 multiply_reduce_fusion
  236.2 1.4 multiply_convert_fusion
  237.7 1.2 fusion.39
  239.0 0.8 select_reduce_fusion.1
  239.8 0.1 copy.80
  240.0 0.1 copy.79
  240.1 1.1 concatenate.17
  241.2 7.6 %copy.81 = bf16[10,2,192,512]{2,3,1,0:T(8,128)(2,1)} copy(bf16[10,2,192,512]{3,2,1,0:T(8,128)(2,1)} %param.26) | data formatting | bytes 7864320 | tf_op args[12]
  248.8 6.1 %copy.82 = bf16[8,192,2,10,64]{1,4,3,2,0:T(8,128)(2,1)} copy(bf16[8,192,2,10,64]{1,4,0,2,3:T(8,128)(2,1)} %bitcast.29) | data formatting | bytes 7864320 | tf_op jit(solution)/shard_map/transpose | solution.py:183
  255.0 7.5 %copy.83 = bf16[8,192,1280]{2,1,0:T(8,128)(2,1)} copy(bf16[8,192,1280]{1,2,0:T(8,128)(2,1)} %bitcast.28) | data formatting | bytes 7864320 | tf_op jit(solution)/shard_map/all_to_all | solution.py:186
  262.5 5.5 all-to-all-start.1
  268.0 145.7 %all-to-all-done.1 = bf16[8,192,1280]{2,1,0:T(8,128)(2,1)} async-done(((bf16[8,192,1280]{2,1,0:T(8,128)(2,1)}), bf16[8,192,1280]{2,1,0:T(8,128)(2,1)}, u32[]{:S(2)}, u32[]{:S(2)}) %all-to-all-start.1) | async-done | bytes 3932192 | tf_op jit(solution)/shard_map/all_to_all | solution.py:186
  413.7 7.3 %all-gather.5.cloned.1.call-done = bf16[2048,1664]{1,0:T(8,128)(2,1)} async-done(((bf16[256,1664]{1,0:T(8,128)(2,1)}), bf16[2048,1664]{1,0:T(8,128)(2,1)}) %all-gather.5.cloned.1.call-update) | async-done | bytes 6815760 | tf_op jit(solution)/shard_map/all_gather | solution.py:251
  421.0 13.9 %fusion = f32[2048,1280]{1,0:T(8,128)} fusion(bf16[1536,1280]{1,0:T(8,128)(2,1)} %bitcast.12, bf16[2048,1664]{1,0:T(8,128)(2,1)} %all-gather.5.cloned.1.call-done), kind=kOutput, calls=%fused_computation.1 | convolution fusion | flops 8053063680 | bytes 20709376 | tf_op jit(solution)/shard_map/dot_general | solution.py:257
  434.9 10.7 %convolution_convert_fusion = bf16[2048,1536]{1,0:T(8,128)(2,1)} fusion(bf16[640,1536]{1,0:T(8,128)(2,1)S(1)} %bitcast.27, f32[2048,1280]{1,0:T(8,128)} %fusion, bf16[2048,1664]{1,0:T(8,128)(2,1)} %all-gather.5.cloned.1.call-done, s32[640]{0:T(1024)S(1)} %add_select_fusion, s32[128]{0:T(128)S(1)} %and_select_fusion, pred[128]{0:T(512)(128)(4,1)S(1)} %iota_compare_fusion.2), kind=kOutput, calls=%fused_computation | convolution fusion | flops 4374560768 | bytes 19270784 | tf_op jit(solution)/shard_map/dot_general | solution.py:259
  445.6 116.3 %reduce-scatter.2.cloned.1.call-done = bf16[256,1536]{1,0:T(8,128)(2,1)} async-done(((bf16[2048,1536]{1,0:T(8,128)(2,1)}), bf16[256,1536]{1,0:T(8,128)(2,1)}) %reduce-scatter.2.cloned.1.call-update) | async-done | bytes 786448 | tf_op jit(solution)/shard_map/reduce_scatter | solution.py:260
  562.0 36.0 %all-reduce.7.cloned.1.call-done = bf16[256,1536]{1,0:T(8,128)(2,1)} async-done(((bf16[256,1536]{1,0:T(8,128)(2,1)}), bf16[256,1536]{1,0:T(8,128)(2,1)}) %all-reduce.7.cloned.1.call-update) | async-done | bytes 786448 | tf_op jit(solution)/shard_map/psum | solution.py:261
  598.0 0.9 copy.90
  598.9 2.1 copy.91
  (52 shorter events, 0.8 us)
Async XLA Ops:
  7.2 427.7 %copy-start = (bf16[10,64,1536]{2,1,0:T(8,128)(2,1)S(1)}, bf16[10,64,1536]{2,1,0:T(8,128)(2,1)}, u32[]{:S(2)}) copy-start(bf16[10,64,1536]{2,1,0:T(8,128)(2,1)} %param.27) | copy-start | bytes 5898244
  7.2 53.4 %all-gather.3.cloned.1.call-start = ((), (), s32[]{:S(2)}) async-start(), calls=%async_computation.3 | async-start | bytes 1769472 | tf_op jit(solution)/shard_map/all_gather | solution.py:205
  8.7 5.0 copy-start.4
  13.5 221.2 %all-reduce.5.cloned.1.call-start = ((), (), s32[]{:S(2)}) async-start(), calls=%async_computation.4 | async-start | bytes 1572864 | tf_op jit(solution)/shard_map/psum | solution.py:230
  17.2 6.5 %copy-start.9 = (s32[4]{0:T(128)S(1)}, s32[4]{0:T(128)}, u32[]{:S(2)}) copy-start(s32[4]{0:T(128)} %param.21) | copy-start | bytes 52
  60.6 1.2 copy-start.1
  61.8 1.4 copy-start.2
  188.7 2.7 copy-start.3
  194.8 4.6 copy-start.10
  199.4 2.0 copy-start.8
  199.4 35.3 %copy-start.5 = (bf16[256,1536]{1,0:T(8,128)(2,1)S(1)}, bf16[256,1536]{1,0:T(8,128)(2,1)}, u32[]{:S(2)}) copy-start(bf16[256,1536]{1,0:T(8,128)(2,1)} %param.14) | copy-start | bytes 2359300
  201.1 37.8 %copy-start.7 = (s32[256,8]{0,1:T(8,128)S(1)}, s32[256,8]{0,1:T(8,128)}, u32[]{:S(2)}) copy-start(s32[256,8]{0,1:T(8,128)} %param.25) | copy-start | bytes 24580
  201.1 219.9 %all-gather.5.cloned.1.call-start = ((), (), s32[]{:S(2)}) async-start(), calls=%async_computation.5 | async-start | bytes 7667712 | tf_op jit(solution)/shard_map/all_gather | solution.py:251
  262.5 151.2 %all-to-all-start.1 = ((bf16[8,192,1280]{2,1,0:T(8,128)(2,1)}), bf16[8,192,1280]{2,1,0:T(8,128)(2,1)}, u32[]{:S(2)}, u32[]{:S(2)}) async-start(bf16[8,192,1280]{2,1,0:T(8,128)(2,1)} %copy.83), calls=%async_computation.1 | async-start | bytes 7864320 | tf_op jit(solution)/shard_map/all_to_all | solution.py:186
  267.9 294.0 %reduce-scatter.2.cloned.1.call-start = ((), (), s32[]{:S(2)}) async-start(), calls=%async_computation.6 | async-start | bytes 7077888 | tf_op jit(solution)/shard_map/reduce_scatter | solution.py:260
  445.6 152.4 %copy-start.6 = (bf16[256,1536]{1,0:T(8,128)(2,1)S(1)}, bf16[256,1536]{1,0:T(8,128)(2,1)}, u32[]{:S(2)}) copy-start(bf16[256,1536]{1,0:T(8,128)(2,1)} %all-reduce.5.cloned.1.call-done) | copy-start | bytes 2359300
  445.6 152.4 %all-reduce.7.cloned.1.call-start = ((), (), s32[]{:S(2)}) async-start(), calls=%async_computation.7 | async-start | bytes 1572864 | tf_op jit(solution)/shard_map/psum | solution.py:261
Sparse Core Ops, SparseCore 0:
  13.6 46.8 all-gather.2
  201.2 33.4 all-reduce.4
  241.4 179.5 all-gather.4
  445.7 116.1 reduce-scatter.1
  564.2 33.7 all-reduce.6

commit v2 on v1

v2 whole, which is shorter than its diff:
```python
import functools

import jax
import jax.numpy as jnp
from jax import lax
from jax.experimental import pallas as pl
from jax.experimental.pallas import tpu as pltpu
from jax.sharding import PartitionSpec as P

HEAD_SIZE = 64
FRESH_TOKENS = 512


EPS = 1e-05
THETA = 10000.0
NEGATIVE = -1e30


def rms_norm(values, gain):
    mean_square = jnp.mean(values * values, axis=-1, keepdims=True)
    return values * lax.rsqrt(mean_square + EPS) * gain.astype(values.dtype)


def apply_rotary(values, positions):
    half_dim = values.shape[-1] // 2
    exponent = jnp.arange(half_dim, dtype=jnp.float32) * (2.0 / values.shape[-1])
    freqs = THETA ** (-exponent)
    angles = positions[:, None] * freqs[None, :]
    cosine = jnp.cos(angles)[:, None, :]
    sine = jnp.sin(angles)[:, None, :]
    first = values[..., :half_dim]
    second = values[..., half_dim:]
    return jnp.concatenate(
        [first * cosine - second * sine, second * cosine + first * sine], axis=-1
    )


def apply_projection(normalized_input, weight):
    return jnp.einsum("td,fd->tf", normalized_input, weight, preferred_element_type=jnp.float32)


def lookup(table, index):
    hits = index[:, None] == jnp.arange(table.shape[0], dtype=jnp.int32)[None, :]
    return jnp.sum(jnp.where(hits, table[None, :], 0), axis=1)


def attend_kernel(group, info, q_ref, k_ref, v_ref, fk_ref, fv_ref, out_ref, peak_ref, sum_ref, acc_ref):
    heads, rows = acc_ref.shape[0], acc_ref.shape[1]
    pairs = k_ref.shape[2]
    columns = q_ref.shape[1]
    dest = pl.program_id(0)
    me = info[0]
    per = FRESH_TOKENS // rows
    length = info[1 + dest // per]
    base = me * (2 * pairs)
    col = lax.broadcasted_iota(jnp.int32, (columns, 128), 0)
    lane = lax.broadcasted_iota(jnp.int32, (columns, 128), 1)
    out_lane = lax.broadcasted_iota(jnp.int32, (rows, 128), 1)
    has_cache = base < length
    has_fresh = (dest // per == me // per) & (dest >= me)
    nt = (((1,), (1,)), ((), ()))

    def pick(g, odd):
        hit = (col == g * HEAD_SIZE + lane - odd * HEAD_SIZE) & (lane // HEAD_SIZE == odd)
        select = jnp.where(hit, HEAD_SIZE ** (-0.5), 0.0).astype(jnp.bfloat16)
        return jnp.dot(q_ref[...], select, preferred_element_type=jnp.float32).astype(jnp.bfloat16)

    @pl.when(jnp.logical_not(has_cache))
    def _():
        peak_ref[...] = jnp.full_like(peak_ref, NEGATIVE)
        sum_ref[...] = jnp.zeros_like(sum_ref)
        acc_ref[...] = jnp.zeros_like(acc_ref)

    @pl.when(has_cache)
    def _():
        even_pos = base + 2 * lax.broadcasted_iota(jnp.int32, (1, pairs), 1)
        even_bias = jnp.where(even_pos < length, 0.0, NEGATIVE)
        odd_bias = jnp.where(even_pos + 1 < length, 0.0, NEGATIVE)
        @pl.loop(0, heads // group)
        def _(j):
            for i in range(group):
                g = j * group + i
                keys = k_ref[0, j]
                values = v_ref[0, j]
                even = lax.dot_general(pick(g, 0), keys, nt, preferred_element_type=jnp.float32) + even_bias
                odd = lax.dot_general(pick(g, 1), keys, nt, preferred_element_type=jnp.float32) + odd_bias
                peak = jnp.max(jnp.maximum(even, odd), axis=1, keepdims=True)
                even = jnp.exp(even - peak)
                odd = jnp.exp(odd - peak)
                total = jnp.sum(even + odd, axis=1, keepdims=True)
                mix_even = jnp.dot(even.astype(jnp.bfloat16), values, preferred_element_type=jnp.float32)
                mix_odd = jnp.dot(odd.astype(jnp.bfloat16), values, preferred_element_type=jnp.float32)
                mixed = jnp.where(out_lane < HEAD_SIZE, mix_even, mix_odd)
                peak_ref[g] = jnp.broadcast_to(peak, (rows, 128))
                sum_ref[g] = jnp.broadcast_to(total, (rows, 128))
                acc_ref[g] = mixed

    @pl.when(has_fresh)
    def _():
        row_q = dest * rows + lax.broadcasted_iota(jnp.int32, (rows, rows), 0)
        row_k = me * rows + lax.broadcasted_iota(jnp.int32, (rows, rows), 1)
        bias = jnp.where(row_k <= row_q, 0.0, NEGATIVE)
        @pl.loop(0, heads // group)
        def _(j):
            for i in range(group):
                g = j * group + i
                score = lax.dot_general(pick(g, 0), fk_ref[j], nt, preferred_element_type=jnp.float32) + bias
                old = peak_ref[g][:, :1]
                peak = jnp.maximum(old, jnp.max(score, axis=1, keepdims=True))
                weight = jnp.exp(score - peak)
                factor = jnp.exp(old - peak)
                total = sum_ref[g][:, :1] * factor + jnp.sum(weight, axis=1, keepdims=True)
                mix = jnp.dot(weight.astype(jnp.bfloat16), fv_ref[j], preferred_element_type=jnp.float32)
                acc_ref[g] = acc_ref[g] * factor + mix
                peak_ref[g] = jnp.broadcast_to(peak, (rows, 128))
                sum_ref[g] = jnp.broadcast_to(total, (rows, 128))

    tail = jnp.zeros((rows, 128), jnp.float32)
    left = None
    for g in range(heads):
        acc = acc_ref[g]
        acc = acc + pltpu.roll(acc, HEAD_SIZE, 1)
        total = sum_ref[g]
        some = total > 0.0
        safe = jnp.where(some, total, 1.0)
        level = jnp.where(some, peak_ref[g] + jnp.log(safe), NEGATIVE)
        high = level.astype(jnp.bfloat16).astype(jnp.float32)
        middle = (level - high).astype(jnp.bfloat16).astype(jnp.float32)
        low = level - high - middle
        tail = jnp.where(out_lane == g, high, tail)
        tail = jnp.where(out_lane == heads + g, middle, tail)
        tail = jnp.where(out_lane == 2 * heads + g, low, tail)
        result = acc / safe
        if g % 2 == 0:
            left = result
        if g % 2 == 1 or g == heads - 1:
            block = jnp.where(out_lane < HEAD_SIZE, left, result)
            out_ref[0, :, g // 2 * 128 : g // 2 * 128 + 128] = block.astype(out_ref.dtype)
    out_ref[0, :, out_ref.shape[2] - 128 :] = tail.astype(out_ref.dtype)


def attend(info, query, keys, values, fresh_key, fresh_value, rows, local_q):
    local_kv, pairs = keys.shape[1], keys.shape[2]
    group = local_q // local_kv
    per = FRESH_TOKENS // rows
    dests = query.shape[0] // rows
    cache_spec = pl.BlockSpec((1, local_kv, pairs, 128), lambda d, info: (d // per, 0, 0, 0))
    fresh_spec = pl.BlockSpec((local_kv, rows, 128), lambda d, info: (0, 0, 0))
    columns = (local_q + 1) // 2 * 128 + 128
    return pl.pallas_call(
        functools.partial(attend_kernel, group),
        grid_spec=pltpu.PrefetchScalarGridSpec(
            num_scalar_prefetch=1,
            grid=(dests,),
            in_specs=[
                pl.BlockSpec((rows, local_q * HEAD_SIZE), lambda d, info: (d, 0)),
                cache_spec,
                cache_spec,
                fresh_spec,
                fresh_spec,
            ],
            out_specs=pl.BlockSpec((1, rows, columns), lambda d, info: (d, 0, 0)),
            scratch_shapes=[pltpu.VMEM((local_q, rows, 128), jnp.float32)] * 3,
        ),
        out_shape=jax.ShapeDtypeStruct((dests, rows, columns), jnp.bfloat16),
        compiler_params=pltpu.CompilerParams(vmem_limit_bytes=40 * 1024 * 1024),
        cost_estimate=pl.CostEstimate(
            flops=8 * query.size * pairs * 2, bytes_accessed=16 << 20, transcendentals=query.size * pairs // 32
        ),
    )(info, query, keys, values, fresh_key, fresh_value)


def swap_cores(values):
    count = lax.axis_size("tp")
    return lax.ppermute(values, "tp", [(i, i ^ 1) for i in range(count)])


def sum_halves(mine, others):
    received = swap_cores(others.astype(jnp.bfloat16)).astype(jnp.float32)
    return (mine + received).astype(jnp.bfloat16)


def sum_chips(values):
    count = lax.axis_size("tp")
    step = 2
    total = values.astype(jnp.float32)
    while step < count:
        sent = total.astype(jnp.bfloat16)
        received = lax.ppermute(sent, "tp", [(i, i ^ step) for i in range(count)])
        total = sent.astype(jnp.float32) + received.astype(jnp.float32)
        step = step * 2
    return total.astype(jnp.bfloat16)


def join_halves(values, core):
    other = swap_cores(values)
    first = jnp.where(core == 0, values, other)
    second = jnp.where(core == 0, other, values)
    return jnp.concatenate([first, second], axis=1)


def per_device(
    tokens,
    norm1_gain,
    w_query,
    key_weight,
    value_weight,
    rotated_key_cache,
    stored_value_cache,
    cache_len,
    w_out,
    norm2_gain,
    w_router,
    expert_ids,
    w_gate_up,
    w_down,
):
    tok_rows, width = tokens.shape
    seq_pos = lax.axis_index("seq")
    tp_pos = lax.axis_index("tp")
    local_q = w_query.shape[0] // HEAD_SIZE
    local_kv = key_weight.shape[0] // HEAD_SIZE
    requests = rotated_key_cache.shape[0]
    span = rotated_key_cache.shape[2] // HEAD_SIZE
    inputs = tokens.astype(jnp.float32)
    devices = lax.axis_size("seq")
    local_experts, _, own_width, hidden_size = w_gate_up.shape
    own_hidden = hidden_size // devices
    units = local_experts * own_hidden
    by_owner = jnp.transpose(
        w_gate_up.reshape(local_experts, 2, own_width, devices, own_hidden), (1, 3, 2, 0, 4)
    ).reshape(2, width, units)
    gate_rows = lax.all_to_all(by_owner[0], "seq", 0, 0, tiled=True)
    normalized_input = rms_norm(inputs, norm1_gain).astype(jnp.bfloat16)
    row_ids = seq_pos * tok_rows + jnp.arange(tok_rows, dtype=jnp.int32)
    owners = row_ids // FRESH_TOKENS
    positions = lookup(cache_len, owners) + row_ids % FRESH_TOKENS
    angle_position = positions.astype(jnp.float32)
    query_vector = apply_rotary(
        apply_projection(normalized_input, w_query).reshape(tok_rows, local_q, HEAD_SIZE),
        angle_position,
    ).astype(jnp.bfloat16)
    fresh_key = apply_rotary(
        apply_projection(normalized_input, key_weight).reshape(tok_rows, local_kv, HEAD_SIZE),
        angle_position,
    ).astype(jnp.bfloat16)
    fresh_value = (
        apply_projection(normalized_input, value_weight)
        .astype(jnp.bfloat16)
        .reshape(tok_rows, local_kv, HEAD_SIZE)
    )
    all_query = lax.all_gather(
        query_vector.reshape(tok_rows, local_q * HEAD_SIZE), "seq", axis=0, tiled=True
    )
    paired = (requests, local_kv, span // 2, 2 * HEAD_SIZE)
    pad = ((0, 0), (0, 0), (0, HEAD_SIZE))
    parts = attend(
        jnp.concatenate([seq_pos[None].astype(jnp.int32), cache_len]),
        all_query,
        rotated_key_cache.reshape(paired),
        stored_value_cache.reshape(paired),
        jnp.pad(jnp.transpose(fresh_key, (1, 0, 2)), pad),
        jnp.pad(jnp.transpose(fresh_value, (1, 0, 2)), pad),
        tok_rows,
        local_q,
    )
    parts, gate_rows = lax.optimization_barrier((parts, gate_rows))
    parts = lax.all_to_all(parts, "seq", 0, 0, tiled=True)
    parts, up_rows = lax.optimization_barrier((parts, by_owner[1]))
    up_rows = lax.all_to_all(up_rows, "seq", 0, 0, tiled=True)
    parts = parts.astype(jnp.float32)
    features = local_q * HEAD_SIZE
    tails = parts.shape[2] - 128
    pieces = parts[:, :, tails : tails + 3 * local_q]
    level = pieces[..., :local_q] + pieces[..., local_q : 2 * local_q] + pieces[..., 2 * local_q :]
    factor = jnp.exp(level - jnp.max(level, axis=0, keepdims=True))
    factor = factor / jnp.sum(factor, axis=0, keepdims=True)
    feature_head = jnp.arange(features, dtype=jnp.int32) // HEAD_SIZE
    widen = (jnp.arange(local_q, dtype=jnp.int32)[:, None] == feature_head[None, :]).astype(jnp.float32)
    factor = jnp.einsum("sth,hf->stf", factor, widen, precision=lax.Precision.HIGHEST)
    heads_out = jnp.sum(parts[:, :, :features] * factor, axis=0).astype(jnp.bfloat16)
    attn_part = jnp.dot(heads_out, w_out, preferred_element_type=jnp.float32)
    core = tp_pos % 2
    half = width // 2
    attn = sum_halves(
        lax.dynamic_slice_in_dim(attn_part, core * half, half, 1),
        lax.dynamic_slice_in_dim(attn_part, (1 - core) * half, half, 1),
    )
    attn = join_halves(sum_chips(attn), core).astype(jnp.float32)
    attn_out = attn.astype(jnp.bfloat16)
    normed2 = rms_norm(inputs + attn, norm2_gain).astype(jnp.bfloat16)
    logits = jnp.dot(normed2, w_router, preferred_element_type=jnp.float32)
    experts_all = w_router.shape[1]
    picked_all = expert_ids[:, :, None] == jnp.arange(experts_all, dtype=jnp.int32)[None, None, :]
    chosen = jnp.sum(jnp.where(picked_all, logits[:, None, :], 0.0), axis=-1)
    gates = jax.nn.softmax(chosen, axis=-1)
    local_ids = tp_pos * local_experts + jnp.arange(local_experts, dtype=jnp.int32)
    picked = expert_ids[:, :, None] == local_ids[None, None, :]
    share = jnp.sum(jnp.where(picked, gates[:, :, None], 0.0), axis=1)
    share_high = lax.reduce_precision(share, 8, 7)
    packed = jnp.concatenate(
        [
            lax.dynamic_slice_in_dim(normed2, core * half, half, 1),
            share_high.astype(jnp.bfloat16),
            (share - share_high).astype(jnp.bfloat16),
            jnp.zeros((tok_rows, 128 - 2 * local_experts), jnp.bfloat16),
        ],
        axis=1,
    )
    packed, up_rows = lax.optimization_barrier((packed, up_rows))
    packed = lax.all_gather(packed, "seq", axis=0, tiled=True)
    others = swap_cores(packed[:, :half])
    unit_expert = jnp.arange(units, dtype=jnp.int32) // own_hidden
    lanes = jnp.arange(128, dtype=jnp.int32)
    spread = (lanes[:, None] % local_experts == unit_expert[None, :]) & (lanes[:, None] < 2 * local_experts)
    share_all = jnp.dot(packed[:, half:], spread.astype(jnp.bfloat16), preferred_element_type=jnp.float32)

    def project(rows):
        mine = lax.dynamic_slice_in_dim(rows, core * half, half, 0)
        theirs = lax.dynamic_slice_in_dim(rows, (1 - core) * half, half, 0)
        return jnp.dot(packed[:, :half], mine, preferred_element_type=jnp.float32) + jnp.dot(
            others, theirs, preferred_element_type=jnp.float32
        )

    hidden = (jax.nn.silu(project(gate_rows)) * project(up_rows) * share_all).astype(jnp.bfloat16)
    down = w_down.reshape(units, width)
    down_mine = lax.dynamic_slice_in_dim(down, core * half, half, 1)
    down_others = lax.dynamic_slice_in_dim(down, (1 - core) * half, half, 1)
    moe_half = sum_halves(
        jnp.dot(hidden, down_mine, preferred_element_type=jnp.float32),
        jnp.dot(hidden, down_others, preferred_element_type=jnp.float32),
    )
    moe_half = lax.psum_scatter(moe_half, "seq", scatter_dimension=0, tiled=True)
    expert_out = join_halves(sum_chips(moe_half.astype(jnp.float32)), core)
    return (attn_out, expert_out)


def solution(mesh):
    return jax.shard_map(
        per_device,
        mesh=mesh,
        in_specs=(
            P("seq", None),
            P(),
            P("tp", None),
            P("tp", None),
            P("tp", None),
            P(None, "tp", "seq"),
            P(None, "tp", "seq"),
            P(),
            P("tp", None),
            P(),
            P(),
            P("seq", None),
            P("tp", None, "seq", None),
            P("tp", "seq", None),
        ),
        out_specs=(P("seq", None), P("seq", None)),
        check_vma=False,
    )
```

time: 609 us -> 471 us (0.77)
  waiting for transfers between devices: 375 us -> 278 us
  blocking collectives: 73 us -> 0 us
  local copies, waits for them, and re-layouts: 38.6 us -> 54.6 us
  starting transfers between devices: 5.84 us -> 19.8 us
    all_to_all x1 -> x0, blocking collectives: 73 us -> none  [per_device(): parts = lax.all_to_all(parts, 'seq', 0, 0, tiled=True).astype(jnp.float32)]
    all_to_all x1 -> x3, waiting for transfers between devices: 146 us -> 75.5 us  [the longest x1 38.4 us: per_device(): parts = lax.all_to_all(parts, 'seq', 0, 0, tiled=True)]
    psum x2 -> x0, waiting for transfers between devices: 68.9 us -> none  [the longest x1 36 us: per_device(): expert_out = lax.psum(moe_part, 'tp')]
    all_gather x1, waiting for transfers between devices: 7.29 us -> 65 us  [per_device(): packed = lax.all_gather(packed, 'seq', axis=0, tiled=True)]
    reduce_scatter x1, waiting for transfers between devices: 116 us -> 72.8 us  [per_device(): lax.psum_scatter(moe_half, 'seq', scatter_dimension=0, tiled=True)]
    ppermute x0 -> x7, waiting for transfers between devices: none -> 20.2 us  [the longest x2 10.2 us: sum_chips(): received = lax.ppermute(sent, 'tp', [(i, i ^ step) for i in range(count)])]
    slice x0 -> x4, local copies, waits for them, and re-layouts: none -> 13.7 us  [the longest x2 9.64 us: per_device(): parts, up_rows = lax.optimization_barrier((parts, by_owner[1]))]
    all_to_all x1 -> x3, starting transfers between devices: 5.46 us -> 16.4 us  [the longest x1 7.39 us: per_device(): gate_rows = lax.all_to_all(by_owner[0], 'seq', 0, 0, tiled=True)]
  transfers between devices with their start and end apart: 6 -> 13, of which waited for: 6 -> 11; matrix products, arithmetic and copies ran while one was open for 5% -> 11% of each run, Pallas kernels for 0% -> 11%
where the time goes in v2:
time: 471 us; the launch traced here: 469 us
  waiting for transfers between devices  278 us (59%)
  local copies, waits for them, and re-layouts  54.6 us (12%)
  Pallas kernels  51.6 us (11%)
  matrix products  37.6 us (8%)
  starting transfers between devices  19.8 us (4%)
  between operations  14.2 us (3%)
  other arithmetic  13.4 us (3%)
    reduce_scatter x1, waiting for transfers between devices, per_device(): lax.psum_scatter(moe_half, 'seq', scatter_dimension=0, tiled=True)  72.8 us
    all_gather x1, waiting for transfers between devices, per_device(): packed = lax.all_gather(packed, 'seq', axis=0, tiled=True)  65 us
    pallas_call x1, Pallas kernels, attend(): pl.pallas_call(functools.partial(attend_kernel, group), grid_spec=pltpu.P...  51.6 us
    all_gather x1, waiting for transfers between devices, per_device(): lax.all_gather(query_vector.reshape(tok_rows, local_q * HEAD_SIZE), 'seq'...  44.2 us
    all_to_all x1, waiting for transfers between devices, per_device(): parts = lax.all_to_all(parts, 'seq', 0, 0, tiled=True)  38.4 us
    all_to_all x1, waiting for transfers between devices, per_device(): up_rows = lax.all_to_all(up_rows, 'seq', 0, 0, tiled=True)  37.1 us
    unnamed x35, local copies, waits for them, and re-layouts  14 us
    dot_general x2, matrix products, project(): jnp.dot(others, theirs, preferred_element_type=jnp.float32)  10.3 us
  transfers between devices with their start and end apart: 13, of which 11 were waited for; matrix products, arithmetic and copies ran while one was open for 11% of the time, Pallas kernels for 11%

profile of v2, /device:TPU:0, one launch (start us, length us, event | category | flops | bytes accessed | tf_op | source)
XLA Modules:
  0.0 469.1 jit_solution(16272813814602164271)
XLA Ops:
  7.2 7.7 %copy.86 = bf16[10,2,192,512]{2,3,1,0:T(8,128)(2,1)} copy(bf16[10,2,192,512]{3,2,1,0:T(8,128)(2,1)} %param.26) | data formatting | bytes 7864320 | tf_op args[12]
  14.9 4.8 %fusion.58 = (bf16[1,8,192,10,64]{2,4,1,0,3:T(8,128)(2,1)}, bf16[1,8,192,10,64]{2,4,1,0,3:T(8,128)(2,1)S(1)}) fusion(bf16[2,8,192,10,64]{2,4,1,0,3:T(8,128)(2,1)} %bitcast.36), kind=kLoop, calls=%fused_computation.116 | loop fusion | bytes 7864320 | tf_op jit(solution)/shard_map/slice | solution.py:269
  19.6 1.8 copy.87
  21.4 4.3 copy.88
  25.7 7.4 %all-to-all-start = ((bf16[8,192,640]{2,1,0:T(8,128)(2,1)}), bf16[8,192,640]{2,1,0:T(8,128)(2,1)}, u32[]{:S(2)}, u32[]{:S(2)}) async-start(bf16[8,192,640]{2,1,0:T(8,128)(2,1)} %copy.88), calls=%async_computation | async-start | bytes 3932160 | tf_op jit(solution)/shard_map/all_to_all | solution.py:233
  33.8 1.9 fusion.53
  38.1 2.6 reshape.236.k_ref
  40.7 3.7 reshape.237.v_ref
  44.4 1.6 fusion.51
  46.8 1.0 copy.96
  47.7 2.3 convolution_convert_fusion.1
  50.1 1.6 copy.85
  51.7 1.0 subtract_convert_fusion
  52.9 0.9 pad.8.fv_ref
  53.9 44.2 %all-gather.3.cloned.1.call-done.q_ref = bf16[2048,384]{1,0:T(8,128)(2,1)} async-done(((bf16[256,384]{1,0:T(8,128)(2,1)}), bf16[2048,384]{1,0:T(8,128)(2,1)}) %all-gather.3.cloned.1.call-update) | async-done | bytes 1572880 | tf_op jit(solution)/shard_map/all_gather | solution.py:252
  98.0 1.2 copy-done.2
  99.3 1.4 copy-done.3
  100.7 51.6 %shard_map.149 = bf16[8,256,512]{2,1,0:T(8,128)(2,1)S(1)} custom-call(s32[5]{0:T(128)S(1)} %pad_add_fusion.info, bf16[2048,384]{1,0:T(8,128)(2,1)S(1)} %copy-done.3, bf16[4,2,512,128]{3,2,1,0:T(8,128)(2,1)S(1)} %reshape.236.k_ref, bf16[4,2,512,128]{3,2,1,0:T(8,128)(2,1)S(1)} %copy-done.2, bf16[2,256,128]{2,1,0:T(8,128)(2,1)S(1)} %pad.7.fk_ref, ...), custom_call_target="tpu_custom_call" | custom-call | flops 6442450944 | bytes 16777216 | tf_op jit(solution)/shard_map/pallas_call | solution.py:150
  152.3 1.3 copy-done.1
  153.6 4.5 all-to-all-start.1
  158.2 4.9 %copy.89 = bf16[1,8,192,10,64]{2,1,4,3,0:T(8,128)(2,1)} copy(bf16[1,8,192,10,64]{2,4,1,0,3:T(8,128)(2,1)} %get-tuple-element.18) | data formatting | bytes 3932160 | tf_op jit(solution)/shard_map/slice | solution.py:269
  163.1 5.2 %squeeze.4 = bf16[1536,640]{0,1:T(8,128)(2,1)} reshape(bf16[1,8,192,10,64]{2,1,4,3,0:T(8,128)(2,1)} %copy.89) | data formatting | bytes 3932160 | tf_op jit(solution)/shard_map/squeeze | solution.py:269
  168.3 38.4 %all-to-all-done.1 = bf16[8,256,512]{2,1,0:T(8,128)(2,1)} async-done(((bf16[8,256,512]{2,1,0:T(8,128)(2,1)}), bf16[8,256,512]{2,1,0:T(8,128)(2,1)}, u32[]{:S(2)}, u32[]{:S(2)}) %all-to-all-start.1) | async-done | bytes 2097184 | tf_op jit(solution)/shard_map/all_to_all | solution.py:268
  206.7 2.2 convert_element_type.101
  209.7 1.7 fusion
  212.7 2.1 collective-permute-done
  214.8 1.8 add_convert_fusion.3
  216.6 1.5 collective-permute-start.1
  218.1 4.0 copy.93
  222.1 4.5 all-to-all-start.2
  226.7 1.3 collective-permute-done.1
  228.0 1.1 add_convert_fusion.2
  233.8 1.5 maximum_maximum_fusion
  235.3 37.1 %all-to-all-done.2 = bf16[8,192,640]{2,1,0:T(8,128)(2,1)} async-done(((bf16[8,192,640]{2,1,0:T(8,128)(2,1)}), bf16[8,192,640]{2,1,0:T(8,128)(2,1)}, u32[]{:S(2)}, u32[]{:S(2)}) %all-to-all-start.2) | async-done | bytes 1966112 | tf_op jit(solution)/shard_map/all_to_all | solution.py:270
  272.4 65.0 %all-gather.5.cloned.1.call-done = bf16[2048,896]{1,0:T(8,128)(2,1)} async-done(((bf16[256,896]{1,0:T(8,128)(2,1)}), bf16[2048,896]{1,0:T(8,128)(2,1)}) %all-gather.5.cloned.1.call-update) | async-done | bytes 3670032 | tf_op jit(solution)/shard_map/all_gather | solution.py:311
  337.5 2.2 slice.66
  341.4 3.9 fusion.11
  345.3 5.8 %fusion.15 = f32[2048,640]{1,0:T(8,128)} fusion(bf16[1536,640]{1,0:T(8,128)(2,1)} %bitcast.10, s32[]{:T(128)S(6)} %select_n.106, bf16[2048,896]{1,0:T(8,128)(2,1)S(1)} %copy-done.6), kind=kOutput, calls=%fused_computation.26 | convolution fusion | flops 2013265920 | bytes 9371652 | tf_op jit(solution)/shard_map/dot_general | solution.py:321
  351.0 3.8 fusion.13
  354.9 6.4 %multiply_convert_fusion = bf16[2048,640]{1,0:T(8,128)(2,1)} fusion(f32[2048,640]{1,0:T(8,128)S(1)} %fusion.18, f32[2048,640]{1,0:T(8,128)S(1)} %fusion.11, f32[2048,640]{1,0:T(8,128)} %fusion.15, f32[2048,640]{1,0:T(8,128)S(1)} %fusion.13, bf16[2048,768]{1,0:T(8,128)(2,1)S(1)} %collective-permute-done.3, bf16[1536,640]{1,0:T(8,128)(2,1)} %bitcast.14, ...), kind=kOutput, calls=%fused_computation.1 | convolution fusion | flops 2025062400 | bytes 27721732 | tf_op jit(solution)/shard_map/dot_general | solution.py:321
  361.3 4.5 convolution_convert_fusion
  365.9 5.6 %collective-permute-done.4 = bf16[2048,768]{1,0:T(8,128)(2,1)S(1)} collective-permute-done((bf16[2048,768]{1,0:T(8,128)(2,1)S(1)}, bf16[2048,768]{1,0:T(8,128)(2,1)S(1)}, u32[]{:S(2)}, u32[]{:S(2)}) %collective-permute-start.4) | collective-permute-done | bytes 3145760 | tf_op jit(solution)/shard_map/ppermute | solution.py:175
  371.6 3.9 add_convert_fusion
  375.5 72.8 %reduce-scatter.2.cloned.1.call-done = bf16[256,768]{1,0:T(8,128)(2,1)} async-done(((bf16[2048,768]{1,0:T(8,128)(2,1)}), bf16[256,768]{1,0:T(8,128)(2,1)}) %reduce-scatter.2.cloned.1.call-update) | async-done | bytes 393232 | tf_op jit(solution)/shard_map/reduce_scatter | solution.py:333
  448.3 1.5 collective-permute-start.5
  449.8 8.9 %collective-permute-done.5 = bf16[256,768]{1,0:T(8,128)(2,1)S(1)} collective-permute-done((bf16[256,768]{1,0:T(8,128)(2,1)}, bf16[256,768]{1,0:T(8,128)(2,1)S(1)}, u32[]{:S(2)}, u32[]{:S(2)}) %collective-permute-start.5) | collective-permute-done | bytes 393248 | tf_op jit(solution)/shard_map/ppermute | solution.py:189
  458.7 1.1 add_convert_fusion.1
  459.9 1.7 collective-permute-done.6
  (90 shorter events, 13.6 us)
Async XLA Ops:
  7.2 354.1 %copy-start = (bf16[10,64,1536]{2,1,0:T(8,128)(2,1)S(1)}, bf16[10,64,1536]{2,1,0:T(8,128)(2,1)}, u32[]{:S(2)}) copy-start(bf16[10,64,1536]{2,1,0:T(8,128)(2,1)} %param.27) | copy-start | bytes 5898244
  25.7 7.5 %copy-start.11 = (bf16[1536]{0:T(1024)(128)(2,1)S(1)}, bf16[1536]{0:T(1024)(128)(2,1)}, u32[]{:S(2)}) copy-start(bf16[1536]{0:T(1024)(128)(2,1)} %param.15) | copy-start | bytes 9220
  25.7 7.5 %copy-start.4 = (bf16[256,1536]{1,0:T(8,128)(2,1)S(1)}, bf16[256,1536]{1,0:T(8,128)(2,1)}, u32[]{:S(2)}) copy-start(bf16[256,1536]{1,0:T(8,128)(2,1)} %param.14) | copy-start | bytes 2359300
  25.7 7.8 %copy-start.13 = (s32[4]{0:T(128)S(1)}, s32[4]{0:T(128)}, u32[]{:S(2)}) copy-start(s32[4]{0:T(128)} %param.21) | copy-start | bytes 52
  25.7 127.9 %all-to-all-start = ((bf16[8,192,640]{2,1,0:T(8,128)(2,1)}), bf16[8,192,640]{2,1,0:T(8,128)(2,1)}, u32[]{:S(2)}, u32[]{:S(2)}) async-start(bf16[8,192,640]{2,1,0:T(8,128)(2,1)} %copy.88), calls=%async_computation | async-start | bytes 3932160 | tf_op jit(solution)/shard_map/all_to_all | solution.py:233
  33.1 64.9 %all-gather.3.cloned.1.call-start = ((), (), s32[]{:S(2)}) async-start(), calls=%async_computation.4 | async-start | bytes 1769472 | tf_op jit(solution)/shard_map/all_gather | solution.py:252
  35.7 8.7 %copy-start.14 = (bf16[128,1536]{1,0:T(8,128)(2,1)S(1)}, bf16[128,1536]{1,0:T(8,128)(2,1)}, u32[]{:S(2)}) copy-start(bf16[128,1536]{1,0:T(8,128)(2,1)} %param.17) | copy-start | bytes 1179652
  98.0 1.2 copy-start.2
  99.3 1.4 copy-start.3
  152.3 1.3 copy-start.1
  153.6 53.1 %all-to-all-start.1 = ((bf16[8,256,512]{2,1,0:T(8,128)(2,1)}), bf16[8,256,512]{2,1,0:T(8,128)(2,1)}, u32[]{:S(2)}, u32[]{:S(2)}) async-start(bf16[8,256,512]{2,1,0:T(8,128)(2,1)} %copy-done.1), calls=%async_computation.1 | async-start | bytes 4194304 | tf_op jit(solution)/shard_map/all_to_all | solution.py:268
  209.7 1.7 copy-start.8
  212.7 2.1 collective-permute-start
  216.6 11.4 %collective-permute-start.1 = (bf16[256,768]{1,0:T(8,128)(2,1)}, bf16[256,768]{1,0:T(8,128)(2,1)S(1)}, u32[]{:S(2)}, u32[]{:S(2)}) collective-permute-start(bf16[256,768]{1,0:T(8,128)(2,1)} %add_convert_fusion.3), channel_id=1, source_target_pairs={{0,2},{1,3},{2,0},{3,1},{4,6},{5,7},{6,4},{7,5},{8,10},{9,11},{10,... | collective-permute-start | bytes 1179656 | tf_op jit(solution)/shard_map/ppermute | solution.py:189
  222.1 7.1 %copy-start.12 = (bf16[1536]{0:T(1024)(128)(2,1)S(1)}, bf16[1536]{0:T(1024)(128)(2,1)}, u32[]{:S(2)}) copy-start(bf16[1536]{0:T(1024)(128)(2,1)} %param.23) | copy-start | bytes 9220
  222.1 8.8 %copy-start.5 = (bf16[256,1536]{1,0:T(8,128)(2,1)S(1)}, bf16[256,1536]{1,0:T(8,128)(2,1)}, u32[]{:S(2)}) copy-start(bf16[256,1536]{1,0:T(8,128)(2,1)} %param.14) | copy-start | bytes 2359300
  222.1 50.2 %all-to-all-start.2 = ((bf16[8,192,640]{2,1,0:T(8,128)(2,1)}), bf16[8,192,640]{2,1,0:T(8,128)(2,1)}, u32[]{:S(2)}, u32[]{:S(2)}) async-start(bf16[8,192,640]{2,1,0:T(8,128)(2,1)} %bitcast.38), calls=%async_computation.2 | async-start | bytes 3932160 | tf_op jit(solution)/shard_map/all_to_all | solution.py:270
  226.6 110.8 %all-gather.5.cloned.1.call-start = ((), (), s32[]{:S(2)}) async-start(), calls=%async_computation.5 | async-start | bytes 4128768 | tf_op jit(solution)/shard_map/all_gather | solution.py:311
  229.1 1.8 collective-permute-start.2
  231.0 1.3 copy-start.9
  231.0 1.6 copy-start.10
  231.3 0.9 copy-start.7
  272.4 175.9 %reduce-scatter.2.cloned.1.call-start = ((), (), s32[]{:S(2)}) async-start(), calls=%async_computation.6 | async-start | bytes 3538944 | tf_op jit(solution)/shard_map/reduce_scatter | solution.py:333
  337.5 3.0 copy-start.6
  339.7 11.3 %collective-permute-start.3 = (bf16[2048,768]{1,0:T(8,128)(2,1)S(1)}, bf16[2048,768]{1,0:T(8,128)(2,1)S(1)}, u32[]{:S(2)}, u32[]{:S(2)}) collective-permute-start(bf16[2048,768]{1,0:T(8,128)(2,1)S(1)} %slice.66), channel_id=1, source_target_pairs={{0,1},{1,0},{2,3},{3,2},{4,5},{5,4},{6,7},{7,6},{8,9},{9,8},{10,11... | collective-permute-start | bytes 9437192 | tf_op jit(solution)/shard_map/ppermute | solution.py:175
  361.3 10.3 %copy-start.15 = (bf16[2048,640]{1,0:T(8,128)(2,1)S(1)}, bf16[2048,640]{1,0:T(8,128)(2,1)}, u32[]{:S(2)}) copy-start(bf16[2048,640]{1,0:T(8,128)(2,1)} %multiply_convert_fusion) | copy-start | bytes 7864324
  365.8 5.7 %collective-permute-start.4 = (bf16[2048,768]{1,0:T(8,128)(2,1)S(1)}, bf16[2048,768]{1,0:T(8,128)(2,1)S(1)}, u32[]{:S(2)}, u32[]{:S(2)}) collective-permute-start(bf16[2048,768]{1,0:T(8,128)(2,1)S(1)} %convolution_convert_fusion), channel_id=1, source_target_pairs={{0,1},{1,0},{2,3},{3,2},{4,5},{5,4},{6,7},{7,6},{8,9},{9,8},{10,11... | collective-permute-start | bytes 9437192 | tf_op jit(solution)/shard_map/ppermute | solution.py:175
  448.3 10.4 %collective-permute-start.5 = (bf16[256,768]{1,0:T(8,128)(2,1)}, bf16[256,768]{1,0:T(8,128)(2,1)S(1)}, u32[]{:S(2)}, u32[]{:S(2)}) collective-permute-start(bf16[256,768]{1,0:T(8,128)(2,1)} %reduce-scatter.2.cloned.1.call-done), channel_id=1, source_target_pairs={{0,2},{1,3},{2,0},{3,1},{4,6},{5,7},{6,4},{7,5},{8,10},{9,11},{10,... | collective-permute-start | bytes 1179656 | tf_op jit(solution)/shard_map/ppermute | solution.py:189
  459.8 1.8 collective-permute-start.6
Sparse Core Ops, SparseCore 0:
  36.7 61.2 all-gather.2
  272.5 64.9 all-gather.4
  375.6 72.6 reduce-scatter.1

commit v3 on v2

--- a/solution.py
+++ b/solution.py
@@ -226,11 +226,6 @@
     devices = lax.axis_size("seq")
     local_experts, _, own_width, hidden_size = w_gate_up.shape
     own_hidden = hidden_size // devices
-    units = local_experts * own_hidden
-    by_owner = jnp.transpose(
-        w_gate_up.reshape(local_experts, 2, own_width, devices, own_hidden), (1, 3, 2, 0, 4)
-    ).reshape(2, width, units)
-    gate_rows = lax.all_to_all(by_owner[0], "seq", 0, 0, tiled=True)
     normalized_input = rms_norm(inputs, norm1_gain).astype(jnp.bfloat16)
     row_ids = seq_pos * tok_rows + jnp.arange(tok_rows, dtype=jnp.int32)
     owners = row_ids // FRESH_TOKENS
@@ -240,6 +235,10 @@
         apply_projection(normalized_input, w_query).reshape(tok_rows, local_q, HEAD_SIZE),
         angle_position,
     ).astype(jnp.bfloat16)
+    units = local_experts * own_hidden
+    by_owner = jnp.transpose(
+        w_gate_up.reshape(local_experts, 2, own_width, devices, own_hidden), (3, 2, 1, 0, 4)
+    ).reshape(width, 2 * units)
     fresh_key = apply_rotary(
         apply_projection(normalized_input, key_weight).reshape(tok_rows, local_kv, HEAD_SIZE),
         angle_position,
@@ -252,6 +251,8 @@
     all_query = lax.all_gather(
         query_vector.reshape(tok_rows, local_q * HEAD_SIZE), "seq", axis=0, tiled=True
     )
+    all_query, by_owner = lax.optimization_barrier((all_query, by_owner))
+    own_gate_up = lax.all_to_all(by_owner, "seq", 0, 0, tiled=True)
     paired = (requests, local_kv, span // 2, 2 * HEAD_SIZE)
     pad = ((0, 0), (0, 0), (0, HEAD_SIZE))
     parts = attend(
@@ -264,10 +265,8 @@
         tok_rows,
         local_q,
     )
-    parts, gate_rows = lax.optimization_barrier((parts, gate_rows))
+    parts, own_gate_up = lax.optimization_barrier((parts, own_gate_up))
     parts = lax.all_to_all(parts, "seq", 0, 0, tiled=True)
-    parts, up_rows = lax.optimization_barrier((parts, by_owner[1]))
-    up_rows = lax.all_to_all(up_rows, "seq", 0, 0, tiled=True)
     parts = parts.astype(jnp.float32)
     features = local_q * HEAD_SIZE
     tails = parts.shape[2] - 128
@@ -307,22 +306,17 @@
         ],
         axis=1,
     )
-    packed, up_rows = lax.optimization_barrier((packed, up_rows))
     packed = lax.all_gather(packed, "seq", axis=0, tiled=True)
     others = swap_cores(packed[:, :half])
     unit_expert = jnp.arange(units, dtype=jnp.int32) // own_hidden
     lanes = jnp.arange(128, dtype=jnp.int32)
     spread = (lanes[:, None] % local_experts == unit_expert[None, :]) & (lanes[:, None] < 2 * local_experts)
     share_all = jnp.dot(packed[:, half:], spread.astype(jnp.bfloat16), preferred_element_type=jnp.float32)
-
-    def project(rows):
-        mine = lax.dynamic_slice_in_dim(rows, core * half, half, 0)
-        theirs = lax.dynamic_slice_in_dim(rows, (1 - core) * half, half, 0)
-        return jnp.dot(packed[:, :half], mine, preferred_element_type=jnp.float32) + jnp.dot(
-            others, theirs, preferred_element_type=jnp.float32
-        )
-
-    hidden = (jax.nn.silu(project(gate_rows)) * project(up_rows) * share_all).astype(jnp.bfloat16)
+    gate_up_mine = lax.dynamic_slice_in_dim(own_gate_up, core * half, half, 0)
+    gate_up_others = lax.dynamic_slice_in_dim(own_gate_up, (1 - core) * half, half, 0)
+    both = jnp.dot(packed[:, :half], gate_up_mine, preferred_element_type=jnp.float32)
+    both = both + jnp.dot(others, gate_up_others, preferred_element_type=jnp.float32)
+    hidden = (jax.nn.silu(both[:, :units]) * both[:, units:] * share_all).astype(jnp.bfloat16)
     down = w_down.reshape(units, width)
     down_mine = lax.dynamic_slice_in_dim(down, core * half, half, 1)
     down_others = lax.dynamic_slice_in_dim(down, (1 - core) * half, half, 1)

time: 471 us -> 431 us (0.915)
  waiting for transfers between devices: 278 us -> 259 us
  starting transfers between devices: 19.8 us -> 12.7 us
  local copies, waits for them, and re-layouts: 54.6 us -> 47.8 us
  matrix products: 37.6 us -> 32.3 us
    all_gather x1, waiting for transfers between devices: 44.2 us -> 21.8 us  [per_device(): lax.all_gather(query_vector.reshape(tok_rows, local_q * HEAD_SIZE), 'seq'...]
    all_to_all x2 -> x1, waiting for transfers between devices: 37.1 us -> 21.6 us  [per_device(): own_gate_up = lax.all_to_all(by_owner, 'seq', 0, 0, tiled=True)]
    slice x4 -> x1, local copies, waits for them, and re-layouts: 13.7 us -> 2.24 us  [per_device(): packed[:, :half]]
    all_to_all x1, waiting for transfers between devices: 38.4 us -> 47.7 us  [per_device(): parts = lax.all_to_all(parts, 'seq', 0, 0, tiled=True)]
    reshape x0 -> x1, local copies, waits for them, and re-layouts: none -> 9.14 us  [per_device(): by_owner = jnp.transpose(w_gate_up.reshape(local_experts, 2, own_width, d...]
    transpose x0 -> x1, local copies, waits for them, and re-layouts: none -> 8.49 us  [per_device(): jnp.transpose(w_gate_up.reshape(local_experts, 2, own_width, devices, own...]
    ppermute x2, waiting for transfers between devices: 10.2 us -> 18.6 us  [sum_chips(): received = lax.ppermute(sent, 'tp', [(i, i ^ step) for i in range(count)])]
    all_to_all x2 -> x1, starting transfers between devices: 11.9 us -> 4.68 us  [per_device(): own_gate_up = lax.all_to_all(by_owner, 'seq', 0, 0, tiled=True)]
  transfers between devices with their start and end apart: 13 -> 12, of which waited for: 11 -> 11; matrix products, arithmetic and copies ran while one was open for 11% -> 10% of each run, Pallas kernels for 11% -> 12%
where the time goes in v3:
time: 431 us; the launch traced here: 430 us
  waiting for transfers between devices  259 us (60%)
  Pallas kernels  51.4 us (12%)
  local copies, waits for them, and re-layouts  47.8 us (11%)
  matrix products  32.3 us (7%)
  between operations  14.3 us (3%)
  starting transfers between devices  12.7 us (3%)
  other arithmetic  11.6 us (3%)
    reduce_scatter x1, waiting for transfers between devices, per_device(): lax.psum_scatter(moe_half, 'seq', scatter_dimension=0, tiled=True)  73 us
    all_gather x1, waiting for transfers between devices, per_device(): packed = lax.all_gather(packed, 'seq', axis=0, tiled=True)  65.9 us
    pallas_call x1, Pallas kernels, attend(): pl.pallas_call(functools.partial(attend_kernel, group), grid_spec=pltpu.P...  51.4 us
    all_to_all x1, waiting for transfers between devices, per_device(): parts = lax.all_to_all(parts, 'seq', 0, 0, tiled=True)  47.7 us
    all_gather x1, waiting for transfers between devices, per_device(): lax.all_gather(query_vector.reshape(tok_rows, local_q * HEAD_SIZE), 'seq'...  21.8 us
    all_to_all x1, waiting for transfers between devices, per_device(): own_gate_up = lax.all_to_all(by_owner, 'seq', 0, 0, tiled=True)  21.6 us
    ppermute x2, waiting for transfers between devices, sum_chips(): received = lax.ppermute(sent, 'tp', [(i, i ^ step) for i in range(count)])  18.6 us
    unnamed x31, local copies, waits for them, and re-layouts  13.8 us
  transfers between devices with their start and end apart: 12, of which 11 were waited for; matrix products, arithmetic and copies ran while one was open for 10% of the time, Pallas kernels for 12%

profile of v3, /device:TPU:0, one launch (start us, length us, event | category | flops | bytes accessed | tf_op | source)
XLA Modules:
  0.0 429.6 jit_solution(15766318790053522782)
XLA Ops:
  7.2 1.5 fusion.6
  8.8 0.7 select_reduce_fusion.2
  9.5 0.7 convert_element_type.96
  10.4 2.1 fusion.48
  12.6 0.8 copy.59
  13.4 7.6 %copy.60 = bf16[10,2,192,512]{2,3,1,0:T(8,128)(2,1)} copy(bf16[10,2,192,512]{3,2,1,0:T(8,128)(2,1)} %param.26) | data formatting | bytes 7864320 | tf_op args[12]
  21.0 8.5 %copy.61 = bf16[8,192,2,10,64]{1,0,4,3,2:T(8,128)(2,1)} copy(bf16[8,192,2,10,64]{1,4,0,2,3:T(8,128)(2,1)} %bitcast.33) | data formatting | bytes 7864320 | tf_op jit(solution)/shard_map/transpose | solution.py:239
  29.5 9.1 %reshape.232 = bf16[1536,1280]{0,1:T(8,128)(2,1)} reshape(bf16[8,192,2,10,64]{1,0,4,3,2:T(8,128)(2,1)} %copy.61) | data formatting | bytes 7864320 | tf_op jit(solution)/shard_map/reshape | solution.py:241
  38.7 21.8 %all-gather.3.cloned.1.call-done.q_ref = bf16[2048,384]{1,0:T(8,128)(2,1)} async-done(((bf16[256,384]{1,0:T(8,128)(2,1)}), bf16[2048,384]{1,0:T(8,128)(2,1)}) %all-gather.3.cloned.1.call-update) | async-done | bytes 1572880 | tf_op jit(solution)/shard_map/all_gather | solution.py:251
  60.5 6.2 %copy.67 = bf16[1536,1280]{1,0:T(8,128)(2,1)} copy(bf16[1536,1280]{0,1:T(8,128)(2,1)} %reshape.232) | data formatting | bytes 7864320 | tf_op jit(solution)/shard_map/optimization_barrier | solution.py:254
  66.7 4.7 %all-to-all-start = ((bf16[8,192,1280]{2,1,0:T(8,128)(2,1)}), bf16[8,192,1280]{2,1,0:T(8,128)(2,1)}, u32[]{:S(2)}, u32[]{:S(2)}) async-start(bf16[8,192,1280]{2,1,0:T(8,128)(2,1)} %bitcast.34), calls=%async_computation | async-start | bytes 7864320 | tf_op jit(solution)/shard_map/all_to_all | solution.py:255
  71.6 1.5 convolution_convert_fusion.1
  73.2 1.5 fusion.46
  75.2 2.6 reshape.233.k_ref
  77.8 3.7 reshape.234.v_ref
  81.6 1.2 copy-done.2
  82.8 1.4 copy-done.3
  84.2 51.4 %shard_map.149 = bf16[8,256,512]{2,1,0:T(8,128)(2,1)S(1)} custom-call(s32[5]{0:T(128)S(1)} %pad_add_fusion.info, bf16[2048,384]{1,0:T(8,128)(2,1)S(1)} %copy-done.3, bf16[4,2,512,128]{3,2,1,0:T(8,128)(2,1)S(1)} %reshape.233.k_ref, bf16[4,2,512,128]{3,2,1,0:T(8,128)(2,1)S(1)} %copy-done.2, bf16[2,256,128]{2,1,0:T(8,128)(2,1)S(1)} %pad.7.fk_ref, ...), custom_call_target="tpu_custom_call" | custom-call | flops 6442450944 | bytes 16777216 | tf_op jit(solution)/shard_map/pallas_call | solution.py:150
  135.6 1.3 copy-done.1
  137.0 21.6 %all-to-all-done = bf16[8,192,1280]{2,1,0:T(8,128)(2,1)} async-done(((bf16[8,192,1280]{2,1,0:T(8,128)(2,1)}), bf16[8,192,1280]{2,1,0:T(8,128)(2,1)}, u32[]{:S(2)}, u32[]{:S(2)}) %all-to-all-start) | async-done | bytes 3932192 | tf_op jit(solution)/shard_map/all_to_all | solution.py:255
  158.6 4.5 %all-to-all-start.1 = ((bf16[8,256,512]{2,1,0:T(8,128)(2,1)}), bf16[8,256,512]{2,1,0:T(8,128)(2,1)}, u32[]{:S(2)}, u32[]{:S(2)}) async-start(bf16[8,256,512]{2,1,0:T(8,128)(2,1)} %copy-done.1), calls=%async_computation.1 | async-start | bytes 4194304 | tf_op jit(solution)/shard_map/all_to_all | solution.py:269
  163.2 47.7 %all-to-all-done.1 = bf16[8,256,512]{2,1,0:T(8,128)(2,1)} async-done(((bf16[8,256,512]{2,1,0:T(8,128)(2,1)}), bf16[8,256,512]{2,1,0:T(8,128)(2,1)}, u32[]{:S(2)}, u32[]{:S(2)}) %all-to-all-start.1) | async-done | bytes 2097184 | tf_op jit(solution)/shard_map/all_to_all | solution.py:269
  210.9 2.2 convert_element_type.101
  213.1 0.6 fusion.51
  213.9 1.7 fusion.2
  215.6 0.6 fusion.54
  216.2 1.1 copy-done.6
  217.5 1.7 collective-permute-done
  219.2 1.2 add_convert_fusion.3
  220.4 1.5 collective-permute-start.1
  221.9 9.7 %collective-permute-done.1 = bf16[256,768]{1,0:T(8,128)(2,1)S(1)} collective-permute-done((bf16[256,768]{1,0:T(8,128)(2,1)S(1)}, bf16[256,768]{1,0:T(8,128)(2,1)S(1)}, u32[]{:S(2)}, u32[]{:S(2)}) %collective-permute-start.1) | collective-permute-done | bytes 393248 | tf_op jit(solution)/shard_map/ppermute | solution.py:189
  231.9 1.6 collective-permute-done.2
  235.3 0.9 maximum_maximum_fusion
  236.3 65.9 %all-gather.5.cloned.1.call-done = bf16[2048,896]{1,0:T(8,128)(2,1)} async-done(((bf16[256,896]{1,0:T(8,128)(2,1)}), bf16[2048,896]{1,0:T(8,128)(2,1)}) %all-gather.5.cloned.1.call-update) | async-done | bytes 3670032 | tf_op jit(solution)/shard_map/all_gather | solution.py:309
  302.2 2.2 slice.61
  304.6 0.6 copy-done.8
  305.2 8.3 %fusion.4 = f32[2048,1280]{1,0:T(8,128)} fusion(bf16[1536,1280]{1,0:T(8,128)(2,1)} %bitcast.10, s32[]{:T(128)S(6)} %select_n.104, bf16[2048,896]{1,0:T(8,128)(2,1)S(1)} %copy-done.8), kind=kOutput, calls=%fused_computation.12 | convolution fusion | flops 4026531840 | bytes 15597572 | tf_op jit(solution)/shard_map/dot_general | solution.py:317
  313.5 7.7 %convolution_add_fusion = f32[2048,1280]{1,0:T(8,128)S(1)} fusion(f32[2048,1280]{1,0:T(8,128)} %fusion.4, bf16[2048,768]{1,0:T(8,128)(2,1)S(1)} %collective-permute-done.3, bf16[1536,1280]{1,0:T(8,128)(2,1)} %bitcast.10, s32[]{:T(128)S(6)} %select_n.105), kind=kOutput, calls=%fused_computation | convolution fusion | flops 4029153280 | bytes 26083332 | tf_op jit(solution)/shard_map/dot_general | solution.py:318
  321.2 1.9 fusion.1
  323.1 2.8 convolution_convert_fusion
  326.1 5.6 %collective-permute-done.4 = bf16[2048,768]{1,0:T(8,128)(2,1)S(1)} collective-permute-done((bf16[2048,768]{1,0:T(8,128)(2,1)S(1)}, bf16[2048,768]{1,0:T(8,128)(2,1)S(1)}, u32[]{:S(2)}, u32[]{:S(2)}) %collective-permute-start.4) | collective-permute-done | bytes 3145760 | tf_op jit(solution)/shard_map/ppermute | solution.py:175
  331.7 4.0 add_convert_fusion
  335.8 73.0 %reduce-scatter.2.cloned.1.call-done = bf16[256,768]{1,0:T(8,128)(2,1)} async-done(((bf16[2048,768]{1,0:T(8,128)(2,1)}), bf16[256,768]{1,0:T(8,128)(2,1)}) %reduce-scatter.2.cloned.1.call-update) | async-done | bytes 393232 | tf_op jit(solution)/shard_map/reduce_scatter | solution.py:327
  408.8 1.5 collective-permute-start.5
  410.3 8.9 %collective-permute-done.5 = bf16[256,768]{1,0:T(8,128)(2,1)S(1)} collective-permute-done((bf16[256,768]{1,0:T(8,128)(2,1)}, bf16[256,768]{1,0:T(8,128)(2,1)S(1)}, u32[]{:S(2)}, u32[]{:S(2)}) %collective-permute-start.5) | collective-permute-done | bytes 393248 | tf_op jit(solution)/shard_map/ppermute | solution.py:189
  419.2 1.1 add_convert_fusion.1
  420.3 1.7 collective-permute-done.6
  422.1 0.9 pad_maximum_fusion.1
  (79 shorter events, 4.0 us)
Async XLA Ops:
  7.2 316.0 %copy-start = (bf16[10,64,1536]{2,1,0:T(8,128)(2,1)S(1)}, bf16[10,64,1536]{2,1,0:T(8,128)(2,1)}, u32[]{:S(2)}) copy-start(bf16[10,64,1536]{2,1,0:T(8,128)(2,1)} %param.27) | copy-start | bytes 5898244
  7.2 53.3 %all-gather.3.cloned.1.call-start = ((), (), s32[]{:S(2)}) async-start(), calls=%async_computation.3 | async-start | bytes 1769472 | tf_op jit(solution)/shard_map/all_gather | solution.py:251
  66.7 4.9 %copy-start.4 = (bf16[256,1536]{1,0:T(8,128)(2,1)S(1)}, bf16[256,1536]{1,0:T(8,128)(2,1)}, u32[]{:S(2)}) copy-start(bf16[256,1536]{1,0:T(8,128)(2,1)} %param.14) | copy-start | bytes 2359300
  66.7 91.9 %all-to-all-start = ((bf16[8,192,1280]{2,1,0:T(8,128)(2,1)}), bf16[8,192,1280]{2,1,0:T(8,128)(2,1)}, u32[]{:S(2)}, u32[]{:S(2)}) async-start(bf16[8,192,1280]{2,1,0:T(8,128)(2,1)} %bitcast.34), calls=%async_computation | async-start | bytes 7864320 | tf_op jit(solution)/shard_map/all_to_all | solution.py:255
  75.0 6.5 %copy-start.13 = (s32[4]{0:T(128)S(1)}, s32[4]{0:T(128)}, u32[]{:S(2)}) copy-start(s32[4]{0:T(128)} %param.21) | copy-start | bytes 52
  81.6 1.2 copy-start.2
  82.8 1.4 copy-start.3
  135.6 1.3 copy-start.1
  158.6 52.3 %all-to-all-start.1 = ((bf16[8,256,512]{2,1,0:T(8,128)(2,1)}), bf16[8,256,512]{2,1,0:T(8,128)(2,1)}, u32[]{:S(2)}, u32[]{:S(2)}) async-start(bf16[8,256,512]{2,1,0:T(8,128)(2,1)} %copy-done.1), calls=%async_computation.1 | async-start | bytes 4194304 | tf_op jit(solution)/shard_map/all_to_all | solution.py:269
  163.1 139.1 %all-gather.5.cloned.1.call-start = ((), (), s32[]{:S(2)}) async-start(), calls=%async_computation.4 | async-start | bytes 4128768 | tf_op jit(solution)/shard_map/all_gather | solution.py:309
  213.9 1.7 copy-start.9
  215.6 16.2 %copy-start.12 = (bf16[1536]{0:T(1024)(128)(2,1)S(1)}, bf16[1536]{0:T(1024)(128)(2,1)}, u32[]{:S(2)}) copy-start(bf16[1536]{0:T(1024)(128)(2,1)} %param.23) | copy-start | bytes 9220
  216.2 1.2 copy-start.6
  217.3 16.2 %copy-start.5 = (bf16[256,1536]{1,0:T(8,128)(2,1)S(1)}, bf16[256,1536]{1,0:T(8,128)(2,1)}, u32[]{:S(2)}) copy-start(bf16[256,1536]{1,0:T(8,128)(2,1)} %param.14) | copy-start | bytes 2359300
  217.4 1.8 collective-permute-start
  220.4 11.2 %collective-permute-start.1 = (bf16[256,768]{1,0:T(8,128)(2,1)S(1)}, bf16[256,768]{1,0:T(8,128)(2,1)S(1)}, u32[]{:S(2)}, u32[]{:S(2)}) collective-permute-start(bf16[256,768]{1,0:T(8,128)(2,1)S(1)} %add_convert_fusion.3), channel_id=1, source_target_pairs={{0,2},{1,3},{2,0},{3,1},{4,6},{5,7},{6,4},{7,5},{8,10},{9,11},{10,... | collective-permute-start | bytes 1179656 | tf_op jit(solution)/shard_map/ppermute | solution.py:189
  231.7 1.8 collective-permute-start.2
  233.5 0.9 copy-start.10
  233.9 2.3 copy-start.7
  233.9 0.9 copy-start.11
  236.2 172.6 %reduce-scatter.2.cloned.1.call-start = ((), (), s32[]{:S(2)}) async-start(), calls=%async_computation.5 | async-start | bytes 3538944 | tf_op jit(solution)/shard_map/reduce_scatter | solution.py:327
  302.2 3.0 copy-start.8
  304.5 9.0 %collective-permute-start.3 = (bf16[2048,768]{1,0:T(8,128)(2,1)S(1)}, bf16[2048,768]{1,0:T(8,128)(2,1)S(1)}, u32[]{:S(2)}, u32[]{:S(2)}) collective-permute-start(bf16[2048,768]{1,0:T(8,128)(2,1)S(1)} %slice.61), channel_id=1, source_target_pairs={{0,1},{1,0},{2,3},{3,2},{4,5},{5,4},{6,7},{7,6},{8,9},{9,8},{10,11... | collective-permute-start | bytes 9437192 | tf_op jit(solution)/shard_map/ppermute | solution.py:175
  326.0 5.7 %collective-permute-start.4 = (bf16[2048,768]{1,0:T(8,128)(2,1)S(1)}, bf16[2048,768]{1,0:T(8,128)(2,1)S(1)}, u32[]{:S(2)}, u32[]{:S(2)}) collective-permute-start(bf16[2048,768]{1,0:T(8,128)(2,1)S(1)} %convolution_convert_fusion), channel_id=1, source_target_pairs={{0,1},{1,0},{2,3},{3,2},{4,5},{5,4},{6,7},{7,6},{8,9},{9,8},{10,11... | collective-permute-start | bytes 9437192 | tf_op jit(solution)/shard_map/ppermute | solution.py:175
  408.8 10.4 %collective-permute-start.5 = (bf16[256,768]{1,0:T(8,128)(2,1)}, bf16[256,768]{1,0:T(8,128)(2,1)S(1)}, u32[]{:S(2)}, u32[]{:S(2)}) collective-permute-start(bf16[256,768]{1,0:T(8,128)(2,1)} %reduce-scatter.2.cloned.1.call-done), channel_id=1, source_target_pairs={{0,2},{1,3},{2,0},{3,1},{4,6},{5,7},{6,4},{7,5},{8,10},{9,11},{10,... | collective-permute-start | bytes 1179656 | tf_op jit(solution)/shard_map/ppermute | solution.py:189
  420.3 1.8 collective-permute-start.6
Sparse Core Ops, SparseCore 0:
  13.6 46.8 all-gather.2
  236.4 65.8 all-gather.4
  335.9 72.8 reduce-scatter.1

commit v4 on v3

--- a/solution.py
+++ b/solution.py
@@ -238,7 +238,7 @@
     units = local_experts * own_hidden
     by_owner = jnp.transpose(
         w_gate_up.reshape(local_experts, 2, own_width, devices, own_hidden), (3, 2, 1, 0, 4)
-    ).reshape(width, 2 * units)
+    ).reshape(devices, own_width, 2 * units)
     fresh_key = apply_rotary(
         apply_projection(normalized_input, key_weight).reshape(tok_rows, local_kv, HEAD_SIZE),
         angle_position,
@@ -252,7 +252,7 @@
         query_vector.reshape(tok_rows, local_q * HEAD_SIZE), "seq", axis=0, tiled=True
     )
     all_query, by_owner = lax.optimization_barrier((all_query, by_owner))
-    own_gate_up = lax.all_to_all(by_owner, "seq", 0, 0, tiled=True)
+    own_gate_up = lax.all_to_all(by_owner, "seq", 0, 0, tiled=True).reshape(width, 2 * units)
     paired = (requests, local_kv, span // 2, 2 * HEAD_SIZE)
     pad = ((0, 0), (0, 0), (0, HEAD_SIZE))
     parts = attend(

time: 431 us -> 432 us (level)
  waiting for transfers between devices: 259 us -> 271 us
  local copies, waits for them, and re-layouts: 47.8 us -> 37.1 us
    all_gather x1, waiting for transfers between devices: 21.8 us -> 33.8 us  [per_device(): lax.all_gather(query_vector.reshape(tok_rows, local_q * HEAD_SIZE), 'seq'...]
    reshape x1 -> x0, local copies, waits for them, and re-layouts: 9.14 us -> none  [per_device(): by_owner = jnp.transpose(w_gate_up.reshape(local_experts, 2, own_width, d...]
  transfers between devices with their start and end apart: 12 -> 12, of which waited for: 11 -> 11; matrix products, arithmetic and copies ran while one was open for 10% -> 7% of each run, Pallas kernels for 12% -> 12%
where the time goes in v4:
time: 432 us; the launch traced here: 431 us
  waiting for transfers between devices  271 us (63%)
  Pallas kernels  51.4 us (12%)
  local copies, waits for them, and re-layouts  37.1 us (9%)
  matrix products  32.3 us (7%)
  between operations  14.3 us (3%)
  starting transfers between devices  12.7 us (3%)
  other arithmetic  11.6 us (3%)
    reduce_scatter x1, waiting for transfers between devices, per_device(): lax.psum_scatter(moe_half, 'seq', scatter_dimension=0, tiled=True)  73 us
    all_gather x1, waiting for transfers between devices, per_device(): packed = lax.all_gather(packed, 'seq', axis=0, tiled=True)  65.9 us
    pallas_call x1, Pallas kernels, attend(): pl.pallas_call(functools.partial(attend_kernel, group), grid_spec=pltpu.P...  51.4 us
    all_to_all x1, waiting for transfers between devices, per_device(): parts = lax.all_to_all(parts, 'seq', 0, 0, tiled=True)  47.5 us
    all_gather x1, waiting for transfers between devices, per_device(): lax.all_gather(query_vector.reshape(tok_rows, local_q * HEAD_SIZE), 'seq'...  33.8 us
    all_to_all x1, waiting for transfers between devices, per_device(): lax.all_to_all(by_owner, 'seq', 0, 0, tiled=True).reshape(width, 2 * units)  21.6 us
    ppermute x2, waiting for transfers between devices, sum_chips(): received = lax.ppermute(sent, 'tp', [(i, i ^ step) for i in range(count)])  18.6 us
    unnamed x31, local copies, waits for them, and re-layouts  13.8 us
  transfers between devices with their start and end apart: 12, of which 11 were waited for; matrix products, arithmetic and copies ran while one was open for 7% of the time, Pallas kernels for 12%

profile of v4, /device:TPU:0, one launch (start us, length us, event | category | flops | bytes accessed | tf_op | source)
XLA Modules:
  0.0 430.7 jit_solution(13506511465783124751)
XLA Ops:
  7.2 1.5 fusion.6
  8.8 0.7 select_reduce_fusion.2
  9.5 0.7 convert_element_type.96
  10.4 2.1 fusion.48
  12.6 0.8 copy.73
  13.4 7.6 %copy.74 = bf16[10,2,192,512]{2,3,1,0:T(8,128)(2,1)} copy(bf16[10,2,192,512]{3,2,1,0:T(8,128)(2,1)} %param.26) | data formatting | bytes 7864320 | tf_op args[12]
  21.0 5.7 %copy.75 = bf16[8,192,2,10,64]{1,4,3,2,0:T(8,128)(2,1)} copy(bf16[8,192,2,10,64]{1,4,0,2,3:T(8,128)(2,1)} %bitcast.30) | data formatting | bytes 7864320 | tf_op jit(solution)/shard_map/transpose | solution.py:239
  26.7 33.8 %all-gather.3.cloned.1.call-done.q_ref = bf16[2048,384]{1,0:T(8,128)(2,1)} async-done(((bf16[256,384]{1,0:T(8,128)(2,1)}), bf16[2048,384]{1,0:T(8,128)(2,1)}) %all-gather.3.cloned.1.call-update) | async-done | bytes 1572880 | tf_op jit(solution)/shard_map/all_gather | solution.py:251
  60.5 7.5 %copy.81 = bf16[8,192,1280]{2,1,0:T(8,128)(2,1)} copy(bf16[8,192,1280]{1,2,0:T(8,128)(2,1)} %bitcast.29) | data formatting | bytes 7864320 | tf_op jit(solution)/shard_map/optimization_barrier | solution.py:254
  68.0 4.7 %all-to-all-start = ((bf16[8,192,1280]{2,1,0:T(8,128)(2,1)}), bf16[8,192,1280]{2,1,0:T(8,128)(2,1)}, u32[]{:S(2)}, u32[]{:S(2)}) async-start(bf16[8,192,1280]{2,1,0:T(8,128)(2,1)} %copy.81), calls=%async_computation | async-start | bytes 7864320 | tf_op jit(solution)/shard_map/all_to_all | solution.py:255
  72.9 1.5 convolution_convert_fusion.1
  74.5 1.5 fusion.46
  76.5 2.6 reshape.234.k_ref
  79.1 3.7 reshape.235.v_ref
  82.9 1.2 copy-done.2
  84.1 1.4 copy-done.3
  85.6 51.4 %shard_map.149 = bf16[8,256,512]{2,1,0:T(8,128)(2,1)S(1)} custom-call(s32[5]{0:T(128)S(1)} %pad_add_fusion.info, bf16[2048,384]{1,0:T(8,128)(2,1)S(1)} %copy-done.3, bf16[4,2,512,128]{3,2,1,0:T(8,128)(2,1)S(1)} %reshape.234.k_ref, bf16[4,2,512,128]{3,2,1,0:T(8,128)(2,1)S(1)} %copy-done.2, bf16[2,256,128]{2,1,0:T(8,128)(2,1)S(1)} %pad.7.fk_ref, ...), custom_call_target="tpu_custom_call" | custom-call | flops 6442450944 | bytes 16777216 | tf_op jit(solution)/shard_map/pallas_call | solution.py:150
  137.0 1.3 copy-done.1
  138.3 21.6 %all-to-all-done = bf16[8,192,1280]{2,1,0:T(8,128)(2,1)} async-done(((bf16[8,192,1280]{2,1,0:T(8,128)(2,1)}), bf16[8,192,1280]{2,1,0:T(8,128)(2,1)}, u32[]{:S(2)}, u32[]{:S(2)}) %all-to-all-start) | async-done | bytes 3932192 | tf_op jit(solution)/shard_map/all_to_all | solution.py:255
  159.9 4.3 %all-to-all-start.1 = ((bf16[8,256,512]{2,1,0:T(8,128)(2,1)}), bf16[8,256,512]{2,1,0:T(8,128)(2,1)}, u32[]{:S(2)}, u32[]{:S(2)}) async-start(bf16[8,256,512]{2,1,0:T(8,128)(2,1)} %copy-done.1), calls=%async_computation.1 | async-start | bytes 4194304 | tf_op jit(solution)/shard_map/all_to_all | solution.py:269
  164.5 47.5 %all-to-all-done.1 = bf16[8,256,512]{2,1,0:T(8,128)(2,1)} async-done(((bf16[8,256,512]{2,1,0:T(8,128)(2,1)}), bf16[8,256,512]{2,1,0:T(8,128)(2,1)}, u32[]{:S(2)}, u32[]{:S(2)}) %all-to-all-start.1) | async-done | bytes 2097184 | tf_op jit(solution)/shard_map/all_to_all | solution.py:269
  212.1 2.2 convert_element_type.101
  214.2 0.6 fusion.51
  215.1 1.7 fusion.2
  216.7 0.6 fusion.54
  217.3 1.1 copy-done.6
  218.6 1.7 collective-permute-done
  220.3 1.2 add_convert_fusion.3
  221.5 1.5 collective-permute-start.1
  223.0 9.7 %collective-permute-done.1 = bf16[256,768]{1,0:T(8,128)(2,1)S(1)} collective-permute-done((bf16[256,768]{1,0:T(8,128)(2,1)S(1)}, bf16[256,768]{1,0:T(8,128)(2,1)S(1)}, u32[]{:S(2)}, u32[]{:S(2)}) %collective-permute-start.1) | collective-permute-done | bytes 393248 | tf_op jit(solution)/shard_map/ppermute | solution.py:189
  233.0 1.6 collective-permute-done.2
  234.7 0.3 multiply_reduce_fusion
  236.5 0.9 maximum_maximum_fusion
  237.4 65.9 %all-gather.5.cloned.1.call-done = bf16[2048,896]{1,0:T(8,128)(2,1)} async-done(((bf16[256,896]{1,0:T(8,128)(2,1)}), bf16[2048,896]{1,0:T(8,128)(2,1)}) %all-gather.5.cloned.1.call-update) | async-done | bytes 3670032 | tf_op jit(solution)/shard_map/all_gather | solution.py:309
  303.4 2.2 slice.61
  305.7 0.6 copy-done.8
  306.3 8.3 %fusion.4 = f32[2048,1280]{1,0:T(8,128)} fusion(bf16[1536,1280]{1,0:T(8,128)(2,1)} %bitcast.10, s32[]{:T(128)S(6)} %select_n.104, bf16[2048,896]{1,0:T(8,128)(2,1)S(1)} %copy-done.8), kind=kOutput, calls=%fused_computation.12 | convolution fusion | flops 4026531840 | bytes 15597572 | tf_op jit(solution)/shard_map/dot_general | solution.py:317
  314.6 7.7 %convolution_add_fusion = f32[2048,1280]{1,0:T(8,128)S(1)} fusion(f32[2048,1280]{1,0:T(8,128)} %fusion.4, bf16[2048,768]{1,0:T(8,128)(2,1)S(1)} %collective-permute-done.3, bf16[1536,1280]{1,0:T(8,128)(2,1)} %bitcast.10, s32[]{:T(128)S(6)} %select_n.105), kind=kOutput, calls=%fused_computation | convolution fusion | flops 4029153280 | bytes 26083332 | tf_op jit(solution)/shard_map/dot_general | solution.py:318
  322.3 1.9 fusion.1
  324.3 2.8 convolution_convert_fusion
  327.2 5.6 %collective-permute-done.4 = bf16[2048,768]{1,0:T(8,128)(2,1)S(1)} collective-permute-done((bf16[2048,768]{1,0:T(8,128)(2,1)S(1)}, bf16[2048,768]{1,0:T(8,128)(2,1)S(1)}, u32[]{:S(2)}, u32[]{:S(2)}) %collective-permute-start.4) | collective-permute-done | bytes 3145760 | tf_op jit(solution)/shard_map/ppermute | solution.py:175
  332.9 4.0 add_convert_fusion
  336.9 73.0 %reduce-scatter.2.cloned.1.call-done = bf16[256,768]{1,0:T(8,128)(2,1)} async-done(((bf16[2048,768]{1,0:T(8,128)(2,1)}), bf16[256,768]{1,0:T(8,128)(2,1)}) %reduce-scatter.2.cloned.1.call-update) | async-done | bytes 393232 | tf_op jit(solution)/shard_map/reduce_scatter | solution.py:327
  409.9 1.5 collective-permute-start.5
  411.4 8.9 %collective-permute-done.5 = bf16[256,768]{1,0:T(8,128)(2,1)S(1)} collective-permute-done((bf16[256,768]{1,0:T(8,128)(2,1)}, bf16[256,768]{1,0:T(8,128)(2,1)S(1)}, u32[]{:S(2)}, u32[]{:S(2)}) %collective-permute-start.5) | collective-permute-done | bytes 393248 | tf_op jit(solution)/shard_map/ppermute | solution.py:189
  420.3 1.1 add_convert_fusion.1
  421.5 1.7 collective-permute-done.6
  423.3 0.9 pad_maximum_fusion.1
  (78 shorter events, 3.8 us)
Async XLA Ops:
  7.2 317.1 %copy-start = (bf16[10,64,1536]{2,1,0:T(8,128)(2,1)S(1)}, bf16[10,64,1536]{2,1,0:T(8,128)(2,1)}, u32[]{:S(2)}) copy-start(bf16[10,64,1536]{2,1,0:T(8,128)(2,1)} %param.27) | copy-start | bytes 5898244
  7.2 53.3 %all-gather.3.cloned.1.call-start = ((), (), s32[]{:S(2)}) async-start(), calls=%async_computation.3 | async-start | bytes 1769472 | tf_op jit(solution)/shard_map/all_gather | solution.py:251
  68.0 4.9 %copy-start.4 = (bf16[256,1536]{1,0:T(8,128)(2,1)S(1)}, bf16[256,1536]{1,0:T(8,128)(2,1)}, u32[]{:S(2)}) copy-start(bf16[256,1536]{1,0:T(8,128)(2,1)} %param.14) | copy-start | bytes 2359300
  68.0 91.9 %all-to-all-start = ((bf16[8,192,1280]{2,1,0:T(8,128)(2,1)}), bf16[8,192,1280]{2,1,0:T(8,128)(2,1)}, u32[]{:S(2)}, u32[]{:S(2)}) async-start(bf16[8,192,1280]{2,1,0:T(8,128)(2,1)} %copy.81), calls=%async_computation | async-start | bytes 7864320 | tf_op jit(solution)/shard_map/all_to_all | solution.py:255
  76.4 6.5 %copy-start.13 = (s32[4]{0:T(128)S(1)}, s32[4]{0:T(128)}, u32[]{:S(2)}) copy-start(s32[4]{0:T(128)} %param.21) | copy-start | bytes 52
  82.9 1.2 copy-start.2
  84.1 1.4 copy-start.3
  137.0 1.3 copy-start.1
  159.9 52.2 %all-to-all-start.1 = ((bf16[8,256,512]{2,1,0:T(8,128)(2,1)}), bf16[8,256,512]{2,1,0:T(8,128)(2,1)}, u32[]{:S(2)}, u32[]{:S(2)}) async-start(bf16[8,256,512]{2,1,0:T(8,128)(2,1)} %copy-done.1), calls=%async_computation.1 | async-start | bytes 4194304 | tf_op jit(solution)/shard_map/all_to_all | solution.py:269
  164.3 139.1 %all-gather.5.cloned.1.call-start = ((), (), s32[]{:S(2)}) async-start(), calls=%async_computation.4 | async-start | bytes 4128768 | tf_op jit(solution)/shard_map/all_gather | solution.py:309
  215.0 1.7 copy-start.9
  216.7 16.2 %copy-start.12 = (bf16[1536]{0:T(1024)(128)(2,1)S(1)}, bf16[1536]{0:T(1024)(128)(2,1)}, u32[]{:S(2)}) copy-start(bf16[1536]{0:T(1024)(128)(2,1)} %param.23) | copy-start | bytes 9220
  217.3 1.2 copy-start.6
  218.5 16.2 %copy-start.5 = (bf16[256,1536]{1,0:T(8,128)(2,1)S(1)}, bf16[256,1536]{1,0:T(8,128)(2,1)}, u32[]{:S(2)}) copy-start(bf16[256,1536]{1,0:T(8,128)(2,1)} %param.14) | copy-start | bytes 2359300
  218.5 1.8 collective-permute-start
  221.5 11.2 %collective-permute-start.1 = (bf16[256,768]{1,0:T(8,128)(2,1)S(1)}, bf16[256,768]{1,0:T(8,128)(2,1)S(1)}, u32[]{:S(2)}, u32[]{:S(2)}) collective-permute-start(bf16[256,768]{1,0:T(8,128)(2,1)S(1)} %add_convert_fusion.3), channel_id=1, source_target_pairs={{0,2},{1,3},{2,0},{3,1},{4,6},{5,7},{6,4},{7,5},{8,10},{9,11},{10,... | collective-permute-start | bytes 1179656 | tf_op jit(solution)/shard_map/ppermute | solution.py:189
  232.8 1.8 collective-permute-start.2
  234.7 0.9 copy-start.10
  235.0 2.3 copy-start.7
  235.1 0.9 copy-start.11
  237.4 172.6 %reduce-scatter.2.cloned.1.call-start = ((), (), s32[]{:S(2)}) async-start(), calls=%async_computation.5 | async-start | bytes 3538944 | tf_op jit(solution)/shard_map/reduce_scatter | solution.py:327
  303.4 3.0 copy-start.8
  305.6 9.0 %collective-permute-start.3 = (bf16[2048,768]{1,0:T(8,128)(2,1)S(1)}, bf16[2048,768]{1,0:T(8,128)(2,1)S(1)}, u32[]{:S(2)}, u32[]{:S(2)}) collective-permute-start(bf16[2048,768]{1,0:T(8,128)(2,1)S(1)} %slice.61), channel_id=1, source_target_pairs={{0,1},{1,0},{2,3},{3,2},{4,5},{5,4},{6,7},{7,6},{8,9},{9,8},{10,11... | collective-permute-start | bytes 9437192 | tf_op jit(solution)/shard_map/ppermute | solution.py:175
  327.1 5.7 %collective-permute-start.4 = (bf16[2048,768]{1,0:T(8,128)(2,1)S(1)}, bf16[2048,768]{1,0:T(8,128)(2,1)S(1)}, u32[]{:S(2)}, u32[]{:S(2)}) collective-permute-start(bf16[2048,768]{1,0:T(8,128)(2,1)S(1)} %convolution_convert_fusion), channel_id=1, source_target_pairs={{0,1},{1,0},{2,3},{3,2},{4,5},{5,4},{6,7},{7,6},{8,9},{9,8},{10,11... | collective-permute-start | bytes 9437192 | tf_op jit(solution)/shard_map/ppermute | solution.py:175
  409.9 10.4 %collective-permute-start.5 = (bf16[256,768]{1,0:T(8,128)(2,1)}, bf16[256,768]{1,0:T(8,128)(2,1)S(1)}, u32[]{:S(2)}, u32[]{:S(2)}) collective-permute-start(bf16[256,768]{1,0:T(8,128)(2,1)} %reduce-scatter.2.cloned.1.call-done), channel_id=1, source_target_pairs={{0,2},{1,3},{2,0},{3,1},{4,6},{5,7},{6,4},{7,5},{8,10},{9,11},{10,... | collective-permute-start | bytes 1179656 | tf_op jit(solution)/shard_map/ppermute | solution.py:189
  421.4 1.8 collective-permute-start.6
Sparse Core Ops, SparseCore 0:
  13.6 46.8 all-gather.2
  237.5 65.8 all-gather.4
  337.0 72.8 reduce-scatter.1
